TPU v7x, 128 devices: a whole 4x4x4 slice. The times are simulated.
128 devices in a mesh: vox: 8 (over y, core), fas: 16 (over z, x).
Axes of the slice: x: 4, y: 4, z: 4, core: 2. Of those that a mesh axis runs over, the one named last changes fastest.
Arguments:
- signal: float32 [128, 6144], P('vox', 'fas'), may hold values from -6 to 6
- initial_weights: float32 [524288], P('fas'), may hold values from 0.1 to 2
- coefficients: bfloat16 [32768, 4096], P(('vox', 'fas')), may hold values from 0 to 0.0234375
- block_rows: int32 [32768], P(('vox', 'fas')), may hold values from 0 to 127, as said below
- block_cols: int32 [32768], P(('vox', 'fas')), may hold values from 0 to 8191, as said below
- block_atoms: int32 [32768, 64], P(('vox', 'fas')), may hold values from 0 to 359
- block_count: int32 [128], P(('vox', 'fas')), may hold values from 64 to 256, as said below
- dictionary: bfloat16 [360, 96], replicated, may hold values from -6 to 6
Outputs:
- weights: float32 [524288], P('fas')
- residual: float32 [128, 6144], P('vox', 'fas')
Inputs may be any that keep to these rules, and one draw needn't show every extreme that they name: Block slots are stored device by device: the device with vox index i and fas index f holds slots (i * 16 + f) * 256 to (i * 16 + f + 1) * 256 - 1, and every block_rows value there lies in i * 16 to (i + 1) * 16 - 1. For the slots of the device with fas index f, every block_cols value lies in f * 512 to (f + 1) * 512 - 1. `block_count`: entry i * 16 + f is the number of live slots of the device with vox index i and fas index f, its first slots; some device has all 256 live.
All inputs are finite; a program needn't handle non-finite values.
Results may differ from a plain program's by a relative error of at most 0.0003.
Values sent between devices are 32-bit elements; how exact they have to be, the bound alone decides.
A program may use at most 128 MiB of HBM per device.

v0:
```python
import jax
import jax.numpy as jnp
from jax import lax
from jax.sharding import PartitionSpec as P

BV = 64
BF = 64
DIRS = 96
ITERS = 5


def local(
    signal,
    initial_weights,
    coefficients,
    block_rows,
    block_cols,
    block_atoms,
    block_count,
    dictionary,
):
    vox_rows = signal.shape[0]
    fas_rows = initial_weights.shape[0] // BF
    slot_total = coefficients.shape[0]
    row_width = BV * DIRS
    fas_place = lax.axis_index("fas")
    rows_local = block_rows - lax.axis_index("vox") * vox_rows
    cols_local = block_cols - fas_place * fas_rows
    live_count = block_count[0]
    atom_table = dictionary[block_atoms]
    coef_view = coefficients.reshape(slot_total, BV, BF)
    group_size = min(256, slot_total)
    group_turns = (live_count + group_size - 1) // group_size
    vox_range = jnp.arange(vox_rows, dtype=jnp.int32)
    fas_range = jnp.arange(fas_rows, dtype=jnp.int32)

    def group_pieces(first_slot):
        live_mask = (first_slot + jnp.arange(group_size, dtype=jnp.int32) < live_count).astype(
            jnp.float32
        )
        return (coef_view, atom_table, rows_local, cols_local, live_mask)

    def forward_partial(values):
        table = values.reshape(fas_rows, BF)

        def forward_accumulate(turn, running):
            coef_blk, atom_blk, rows_blk, cols_blk, live_mask = group_pieces(turn * group_size)
            scaled = coef_blk.astype(jnp.float32) * table[cols_blk][:, None, :]
            image_blk = jnp.einsum(
                "kvj,kjd->kvd",
                scaled,
                atom_blk.astype(jnp.float32),
                precision=lax.Precision.HIGHEST,
                preferred_element_type=jnp.float32,
            )
            selector = (rows_blk[:, None] == vox_range[None, :]).astype(jnp.float32) * live_mask[
                :, None
            ]
            added = jnp.dot(
                selector.T,
                image_blk.reshape(group_size, row_width),
                precision=lax.Precision.HIGHEST,
                preferred_element_type=jnp.float32,
            )
            return running + added

        start = jnp.zeros((vox_rows, row_width), jnp.float32)
        return lax.fori_loop(0, group_turns, forward_accumulate, start)

    def backward_partial(rows_view):

        def backward_accumulate(turn, running):
            coef_blk, atom_blk, rows_blk, cols_blk, live_mask = group_pieces(turn * group_size)
            gathered = rows_view[rows_blk]
            inner = jnp.einsum(
                "kvj,kvd->kjd",
                coef_blk.astype(jnp.float32),
                gathered,
                precision=lax.Precision.HIGHEST,
                preferred_element_type=jnp.float32,
            )
            contrib = jnp.sum(atom_blk.astype(jnp.float32) * inner, axis=-1)
            selector = (cols_blk[:, None] == fas_range[None, :]).astype(jnp.float32) * live_mask[
                :, None
            ]
            added = jnp.dot(
                selector.T,
                contrib,
                precision=lax.Precision.HIGHEST,
                preferred_element_type=jnp.float32,
            )
            return running + added

        start = jnp.zeros((fas_rows, BF), jnp.float32)
        running = lax.fori_loop(0, group_turns, backward_accumulate, start)
        return running.reshape(-1)

    def collect(partial_value):
        return lax.psum_scatter(partial_value, "fas", scatter_dimension=1, tiled=True)

    weights = initial_weights
    residual = collect(forward_partial(weights)) - signal
    for sweep in range(ITERS):
        whole_rows = lax.all_gather(residual, "fas", axis=1, tiled=True)
        gradient = lax.psum(backward_partial(whole_rows.reshape(vox_rows, BV, DIRS)), "vox")
        projected = jnp.where((weights > 0) | (gradient < 0), gradient, 0.0)
        image_pred = collect(forward_partial(projected))
        image_local = jnp.sum(image_pred * image_pred)
        grad_sq = lax.psum(jnp.sum(projected * projected), "fas")
        image_sq = lax.psum(image_local, ("vox", "fas"))
        step_size = grad_sq / (image_sq + 1e-06)
        weights = jnp.maximum(weights - step_size * projected, 0.0)
        residual = collect(forward_partial(weights)) - signal
    return (weights, residual)


def solution(mesh):
    placed = (
        P("vox", "fas"),
        P("fas"),
        P(("vox", "fas"), None),
        P(("vox", "fas")),
        P(("vox", "fas")),
        P(("vox", "fas"), None),
        P(("vox", "fas")),
        P(),
    )
    return jax.shard_map(
        local, mesh=mesh, in_specs=placed, out_specs=(P("fas"), P("vox", "fas")), check_vma=False
    )
```

profile of v0, /device:TPU:0, one launch (start us, length us, event | category | flops | bytes accessed | tf_op | source)
XLA Modules:
  0.0 2227.8 jit_solution(15539309578874618926)
XLA Ops:
  18.6 57.4 %gather_fusion = bf16[16384,96]{1,0:T(8,128)(2,1)} fusion(bf16[360,96]{1,0:T(8,128)(2,1)S(1)} %copy.28, s32[16384]{0:T(1024)S(1)} %broadcast_clamp_fusion), kind=kCustom, calls=%fused_computation | custom fusion | bytes 6356992 | tf_op jit(solution)/shard_map/gather | solution.py:30
  76.7 27.9 %while.208 = (s32[]{:T(128)}, f32[16,6144]{1,0:T(8,128)S(1)}, s32[]{:T(128)}, s32[256]{0:T(256)S(1)}, s32[]{:T(128)}, /*index=5*/bf16[256,64,64]{2,1,0:T(8,128)(...) while((s32[]{:T(128)}, f32[16,6144]{1,0:T(8,128)S(1)}, ...), condition=%wide.region_1.2_spmd.clone, body=%wide.region_0.1_spmd.clone.sunk | while | flops 1512153856 | bytes 31263864 | solution.py:68
  105.5 74.2 %reduce-scatter.12.cloned.1.call-done = f32[16,384]{1,0:T(8,128)} async-done(((f32[16,6144]{1,0:T(8,128)}), f32[16,384]{1,0:T(8,128)}) %reduce-scatter.12.cloned.1.call-update) | async-done | bytes 24592 | tf_op jit(solution)/shard_map/reduce_scatter | solution.py:99
  180.4 23.6 %all_gather.15 = f32[16,6144]{1,0:T(8,128)S(1)} all-gather(f32[16,384]{1,0:T(8,128)S(1)} %sub.58), channel_id=1, replica_groups=mesh['vox'=8,'fas'=16] {'fas'}, dimensions={1}, use_global_device_ids=true | all-gather | bytes 417792 | tf_op jit(solution)/shard_map/all_gather | solution.py:104
  208.5 13.4 fusion.156
  224.2 58.1 %all-reduce.6.cloned.1.call-done = f32[32768]{0:T(1024)} async-done(((f32[32768]{0:T(1024)}), f32[32768]{0:T(1024)}) %all-reduce.6.cloned.1.call-update) | async-done | bytes 131088 | tf_op jit(solution)/shard_map/psum | solution.py:105
  284.7 28.3 %while.210 = (s32[]{:T(128)}, f32[16,6144]{1,0:T(8,128)S(1)}, s32[]{:T(128)}, s32[256]{0:T(256)S(1)}, s32[]{:T(128)}, /*index=5*/bf16[256,64,64]{2,1,0:T(8,128)(...) while((s32[]{:T(128)}, f32[16,6144]{1,0:T(8,128)S(1)}, ...), condition=%wide.region_10.11_spmd.clone, body=%wide.region_9.10_spmd.clone.sunk | while | flops 1512153856 | bytes 31263864 | solution.py:68
  313.8 70.8 %reduce-scatter.14.cloned.1.call-done = f32[16,384]{1,0:T(8,128)} async-done(((f32[16,6144]{1,0:T(8,128)}), f32[16,384]{1,0:T(8,128)}) %reduce-scatter.14.cloned.1.call-update) | async-done | bytes 24592 | tf_op jit(solution)/shard_map/reduce_scatter | solution.py:99
  386.0 38.8 %psum.106 = f32[]{:T(128)} all-reduce(f32[]{:T(128)} %get-tuple-element.2460), channel_id=1, replica_groups=mesh['vox'=8,'fas'=16] {'fas'}, use_global_device_ids=true, to_apply=%region_8.9 | all-reduce | flops 1 | bytes 8 | tf_op jit(solution)/shard_map/psum | solution.py:109
  424.8 62.7 %psum.107 = f32[]{:T(128)} all-reduce(f32[]{:T(128)} %multiply_reduce_fusion.9), channel_id=1, replica_groups=mesh['vox'=8,'fas'=16] {'vox','fas'}, use_global_device_ids=true, to_apply=%region_13.14 | all-reduce | flops 1 | bytes 8 | tf_op jit(solution)/shard_map/psum | solution.py:110
  489.7 28.1 %while.211 = (s32[]{:T(128)}, f32[16,6144]{1,0:T(8,128)S(1)}, s32[]{:T(128)}, s32[256]{0:T(256)S(1)}, s32[]{:T(128)}, /*index=5*/bf16[256,64,64]{2,1,0:T(8,128)(...) while((s32[]{:T(128)}, f32[16,6144]{1,0:T(8,128)S(1)}, ...), condition=%wide.region_15.16_spmd.clone, body=%wide.region_14.15_spmd.clone.sunk | while | flops 1512153856 | bytes 31263864 | solution.py:68
  518.6 69.0 %reduce-scatter.16.cloned.1.call-done = f32[16,384]{1,0:T(8,128)} async-done(((f32[16,6144]{1,0:T(8,128)}), f32[16,384]{1,0:T(8,128)}) %reduce-scatter.16.cloned.1.call-update) | async-done | bytes 24592 | tf_op jit(solution)/shard_map/reduce_scatter | solution.py:99
  588.4 23.6 %all_gather.16 = f32[16,6144]{1,0:T(8,128)S(1)} all-gather(f32[16,384]{1,0:T(8,128)S(1)} %sub.60), channel_id=1, replica_groups=mesh['vox'=8,'fas'=16] {'fas'}, dimensions={1}, use_global_device_ids=true | all-gather | bytes 417792 | tf_op jit(solution)/shard_map/all_gather | solution.py:104
  616.5 13.4 fusion.157
  632.2 58.0 %all-reduce.8.cloned.1.call-done = f32[32768]{0:T(1024)} async-done(((f32[32768]{0:T(1024)}), f32[32768]{0:T(1024)}) %all-reduce.8.cloned.1.call-update) | async-done | bytes 131088 | tf_op jit(solution)/shard_map/psum | solution.py:105
  692.6 28.2 %while.213 = (s32[]{:T(128)}, f32[16,6144]{1,0:T(8,128)S(1)}, s32[]{:T(128)}, s32[256]{0:T(256)S(1)}, s32[]{:T(128)}, /*index=5*/bf16[256,64,64]{2,1,0:T(8,128)(...) while((s32[]{:T(128)}, f32[16,6144]{1,0:T(8,128)S(1)}, ...), condition=%wide.region_24.25_spmd.clone, body=%wide.region_23.24_spmd.clone.sunk | while | flops 1512153856 | bytes 31263864 | solution.py:68
  721.6 70.8 %reduce-scatter.18.cloned.1.call-done = f32[16,384]{1,0:T(8,128)} async-done(((f32[16,6144]{1,0:T(8,128)}), f32[16,384]{1,0:T(8,128)}) %reduce-scatter.18.cloned.1.call-update) | async-done | bytes 24592 | tf_op jit(solution)/shard_map/reduce_scatter | solution.py:99
  793.8 38.8 %psum.109 = f32[]{:T(128)} all-reduce(f32[]{:T(128)} %get-tuple-element.2458), channel_id=1, replica_groups=mesh['vox'=8,'fas'=16] {'fas'}, use_global_device_ids=true, to_apply=%region_22.23 | all-reduce | flops 1 | bytes 8 | tf_op jit(solution)/shard_map/psum | solution.py:109
  832.5 62.7 %psum.110 = f32[]{:T(128)} all-reduce(f32[]{:T(128)} %multiply_reduce_fusion.8), channel_id=1, replica_groups=mesh['vox'=8,'fas'=16] {'vox','fas'}, use_global_device_ids=true, to_apply=%region_27.28 | all-reduce | flops 1 | bytes 8 | tf_op jit(solution)/shard_map/psum | solution.py:110
  897.5 28.4 %while.214 = (s32[]{:T(128)}, f32[16,6144]{1,0:T(8,128)S(1)}, s32[]{:T(128)}, s32[256]{0:T(256)S(1)}, s32[]{:T(128)}, /*index=5*/bf16[256,64,64]{2,1,0:T(8,128)(...) while((s32[]{:T(128)}, f32[16,6144]{1,0:T(8,128)S(1)}, ...), condition=%wide.region_29.30_spmd.clone, body=%wide.region_28.29_spmd.clone.sunk | while | flops 1512153856 | bytes 31263864 | solution.py:68
  926.7 69.0 %reduce-scatter.20.cloned.1.call-done = f32[16,384]{1,0:T(8,128)} async-done(((f32[16,6144]{1,0:T(8,128)}), f32[16,384]{1,0:T(8,128)}) %reduce-scatter.20.cloned.1.call-update) | async-done | bytes 24592 | tf_op jit(solution)/shard_map/reduce_scatter | solution.py:99
  996.5 23.5 %all_gather.17 = f32[16,6144]{1,0:T(8,128)S(1)} all-gather(f32[16,384]{1,0:T(8,128)S(1)} %sub.62), channel_id=1, replica_groups=mesh['vox'=8,'fas'=16] {'fas'}, dimensions={1}, use_global_device_ids=true | all-gather | bytes 417792 | tf_op jit(solution)/shard_map/all_gather | solution.py:104
  1024.5 13.4 fusion.158
  1040.2 57.9 %all-reduce.10.cloned.1.call-done = f32[32768]{0:T(1024)} async-done(((f32[32768]{0:T(1024)}), f32[32768]{0:T(1024)}) %all-reduce.10.cloned.1.call-update) | async-done | bytes 131088 | tf_op jit(solution)/shard_map/psum | solution.py:105
  1100.6 28.1 %while.216 = (s32[]{:T(128)}, f32[16,6144]{1,0:T(8,128)S(1)}, s32[]{:T(128)}, s32[256]{0:T(256)S(1)}, s32[]{:T(128)}, /*index=5*/bf16[256,64,64]{2,1,0:T(8,128)(...) while((s32[]{:T(128)}, f32[16,6144]{1,0:T(8,128)S(1)}, ...), condition=%wide.region_38.39_spmd.clone, body=%wide.region_37.38_spmd.clone.sunk | while | flops 1512153856 | bytes 31263864 | solution.py:68
  1129.5 70.8 %reduce-scatter.22.cloned.1.call-done = f32[16,384]{1,0:T(8,128)} async-done(((f32[16,6144]{1,0:T(8,128)}), f32[16,384]{1,0:T(8,128)}) %reduce-scatter.22.cloned.1.call-update) | async-done | bytes 24592 | tf_op jit(solution)/shard_map/reduce_scatter | solution.py:99
  1201.7 38.8 %psum.112 = f32[]{:T(128)} all-reduce(f32[]{:T(128)} %get-tuple-element.2456), channel_id=1, replica_groups=mesh['vox'=8,'fas'=16] {'fas'}, use_global_device_ids=true, to_apply=%region_36.37 | all-reduce | flops 1 | bytes 8 | tf_op jit(solution)/shard_map/psum | solution.py:109
  1240.5 62.7 %psum.113 = f32[]{:T(128)} all-reduce(f32[]{:T(128)} %multiply_reduce_fusion.7), channel_id=1, replica_groups=mesh['vox'=8,'fas'=16] {'vox','fas'}, use_global_device_ids=true, to_apply=%region_41.42 | all-reduce | flops 1 | bytes 8 | tf_op jit(solution)/shard_map/psum | solution.py:110
  1305.5 28.3 %while.217 = (s32[]{:T(128)}, f32[16,6144]{1,0:T(8,128)S(1)}, s32[]{:T(128)}, s32[256]{0:T(256)S(1)}, s32[]{:T(128)}, /*index=5*/bf16[256,64,64]{2,1,0:T(8,128)(...) while((s32[]{:T(128)}, f32[16,6144]{1,0:T(8,128)S(1)}, ...), condition=%wide.region_43.44_spmd.clone, body=%wide.region_42.43_spmd.clone.sunk | while | flops 1512153856 | bytes 31263864 | solution.py:68
  1334.6 69.0 %reduce-scatter.24.cloned.1.call-done = f32[16,384]{1,0:T(8,128)} async-done(((f32[16,6144]{1,0:T(8,128)}), f32[16,384]{1,0:T(8,128)}) %reduce-scatter.24.cloned.1.call-update) | async-done | bytes 24592 | tf_op jit(solution)/shard_map/reduce_scatter | solution.py:99
  1404.3 23.5 %all_gather.18 = f32[16,6144]{1,0:T(8,128)S(1)} all-gather(f32[16,384]{1,0:T(8,128)S(1)} %sub.64), channel_id=1, replica_groups=mesh['vox'=8,'fas'=16] {'fas'}, dimensions={1}, use_global_device_ids=true | all-gather | bytes 417792 | tf_op jit(solution)/shard_map/all_gather | solution.py:104
  1432.4 13.4 fusion.159
  1448.1 58.0 %all-reduce.12.cloned.1.call-done = f32[32768]{0:T(1024)} async-done(((f32[32768]{0:T(1024)}), f32[32768]{0:T(1024)}) %all-reduce.12.cloned.1.call-update) | async-done | bytes 131088 | tf_op jit(solution)/shard_map/psum | solution.py:105
  1508.5 28.1 %while.219 = (s32[]{:T(128)}, f32[16,6144]{1,0:T(8,128)S(1)}, s32[]{:T(128)}, s32[256]{0:T(256)S(1)}, s32[]{:T(128)}, /*index=5*/bf16[256,64,64]{2,1,0:T(8,128)(...) while((s32[]{:T(128)}, f32[16,6144]{1,0:T(8,128)S(1)}, ...), condition=%wide.region_52.53_spmd.clone, body=%wide.region_51.52_spmd.clone.sunk | while | flops 1512153856 | bytes 31263864 | solution.py:68
  1537.5 70.8 %reduce-scatter.26.cloned.1.call-done = f32[16,384]{1,0:T(8,128)} async-done(((f32[16,6144]{1,0:T(8,128)}), f32[16,384]{1,0:T(8,128)}) %reduce-scatter.26.cloned.1.call-update) | async-done | bytes 24592 | tf_op jit(solution)/shard_map/reduce_scatter | solution.py:99
  1609.7 38.8 %psum.115 = f32[]{:T(128)} all-reduce(f32[]{:T(128)} %get-tuple-element.2454), channel_id=1, replica_groups=mesh['vox'=8,'fas'=16] {'fas'}, use_global_device_ids=true, to_apply=%region_50.51 | all-reduce | flops 1 | bytes 8 | tf_op jit(solution)/shard_map/psum | solution.py:109
  1648.5 62.8 %psum.116 = f32[]{:T(128)} all-reduce(f32[]{:T(128)} %multiply_reduce_fusion.6), channel_id=1, replica_groups=mesh['vox'=8,'fas'=16] {'vox','fas'}, use_global_device_ids=true, to_apply=%region_55.56 | all-reduce | flops 1 | bytes 8 | tf_op jit(solution)/shard_map/psum | solution.py:110
  1713.5 28.3 %while.220 = (s32[]{:T(128)}, f32[16,6144]{1,0:T(8,128)S(1)}, s32[]{:T(128)}, s32[256]{0:T(256)S(1)}, s32[]{:T(128)}, /*index=5*/bf16[256,64,64]{2,1,0:T(8,128)(...) while((s32[]{:T(128)}, f32[16,6144]{1,0:T(8,128)S(1)}, ...), condition=%wide.region_57.58_spmd.clone, body=%wide.region_56.57_spmd.clone.sunk | while | flops 1512153856 | bytes 31263864 | solution.py:68
  1742.6 69.0 %reduce-scatter.28.cloned.1.call-done = f32[16,384]{1,0:T(8,128)} async-done(((f32[16,6144]{1,0:T(8,128)}), f32[16,384]{1,0:T(8,128)}) %reduce-scatter.28.cloned.1.call-update) | async-done | bytes 24592 | tf_op jit(solution)/shard_map/reduce_scatter | solution.py:99
  1812.4 23.5 %all_gather.19 = f32[16,6144]{1,0:T(8,128)S(1)} all-gather(f32[16,384]{1,0:T(8,128)S(1)} %sub.66), channel_id=1, replica_groups=mesh['vox'=8,'fas'=16] {'fas'}, dimensions={1}, use_global_device_ids=true | all-gather | bytes 417792 | tf_op jit(solution)/shard_map/all_gather | solution.py:104
  1840.4 13.4 fusion.160
  1856.1 58.0 %all-reduce.14.cloned.1.call-done = f32[32768]{0:T(1024)} async-done(((f32[32768]{0:T(1024)}), f32[32768]{0:T(1024)}) %all-reduce.14.cloned.1.call-update) | async-done | bytes 131088 | tf_op jit(solution)/shard_map/psum | solution.py:105
  1916.6 28.1 %while.222 = (s32[]{:T(128)}, f32[16,6144]{1,0:T(8,128)S(1)}, s32[]{:T(128)}, s32[256]{0:T(256)S(1)}, s32[]{:T(128)}, /*index=5*/bf16[256,64,64]{2,1,0:T(8,128)(...) while((s32[]{:T(128)}, f32[16,6144]{1,0:T(8,128)S(1)}, ...), condition=%wide.region_66.67_spmd.clone, body=%wide.region_65.66_spmd.clone.sunk | while | flops 1512153856 | bytes 31263864 | solution.py:68
  1945.5 70.8 %reduce-scatter.30.cloned.1.call-done = f32[16,384]{1,0:T(8,128)} async-done(((f32[16,6144]{1,0:T(8,128)}), f32[16,384]{1,0:T(8,128)}) %reduce-scatter.30.cloned.1.call-update) | async-done | bytes 24592 | tf_op jit(solution)/shard_map/reduce_scatter | solution.py:99
  2017.7 38.8 %psum.118 = f32[]{:T(128)} all-reduce(f32[]{:T(128)} %get-tuple-element.2452), channel_id=1, replica_groups=mesh['vox'=8,'fas'=16] {'fas'}, use_global_device_ids=true, to_apply=%region_64.65 | all-reduce | flops 1 | bytes 8 | tf_op jit(solution)/shard_map/psum | solution.py:109
  2056.5 62.7 %psum.119 = f32[]{:T(128)} all-reduce(f32[]{:T(128)} %multiply_reduce_fusion.5), channel_id=1, replica_groups=mesh['vox'=8,'fas'=16] {'vox','fas'}, use_global_device_ids=true, to_apply=%region_69.70 | all-reduce | flops 1 | bytes 8 | tf_op jit(solution)/shard_map/psum | solution.py:110
  2121.5 28.2 %while.223 = (s32[]{:T(128)}, f32[16,6144]{1,0:T(8,128)S(1)}, s32[]{:T(128)}, s32[256]{0:T(256)S(1)}, s32[]{:T(128)}, /*index=5*/bf16[256,64,64]{2,1,0:T(8,128)(...) while((s32[]{:T(128)}, f32[16,6144]{1,0:T(8,128)S(1)}, ...), condition=%wide.region_71.72_spmd.clone, body=%wide.region_70.71_spmd.clone.sunk | while | flops 1512153856 | bytes 31263864 | solution.py:68
  2150.4 69.0 %reduce-scatter.32.cloned.1.call-done = f32[16,384]{1,0:T(8,128)} async-done(((f32[16,6144]{1,0:T(8,128)}), f32[16,384]{1,0:T(8,128)}) %reduce-scatter.32.cloned.1.call-update) | async-done | bytes 24592 | tf_op jit(solution)/shard_map/reduce_scatter | solution.py:99
  (217 shorter events, 395.2 us)
Async XLA Ops:
  7.2 10.8 copy-start.15
  7.2 11.1 copy-start.14
  7.2 11.2 copy-start.16
  7.2 11.2 copy-start.11
  7.2 172.5 %reduce-scatter.12.cloned.1.call-start = ((), (), s32[]{:S(2)}) async-start(), calls=%async_computation.11 | async-start | bytes 417792 | tf_op jit(solution)/shard_map/reduce_scatter | solution.py:99
  18.5 58.1 %copy-start.17 = (s32[256]{0:T(256)S(1)}, s32[256]{0:T(256)}, u32[]{:S(2)}) copy-start(s32[256]{0:T(256)} %param.43) | copy-start | bytes 3076
  76.7 103.0 %copy-start.12 = (f32[16,384]{1,0:T(8,128)S(1)}, f32[16,384]{1,0:T(8,128)}, u32[]{:S(2)}) copy-start(f32[16,384]{1,0:T(8,128)} %param.40) | copy-start | bytes 73732
  104.6 0.7 copy-start.1
  105.4 176.8 %all-reduce.6.cloned.1.call-start = ((), (), s32[]{:S(2)}) async-start(), calls=%async_computation.12 | async-start | bytes 262144 | tf_op jit(solution)/shard_map/psum | solution.py:105
  224.1 160.4 %reduce-scatter.14.cloned.1.call-start = ((), (), s32[]{:S(2)}) async-start(), calls=%async_computation.13 | async-start | bytes 417792 | tf_op jit(solution)/shard_map/reduce_scatter | solution.py:99
  313.0 0.7 copy-start.2
  313.8 273.9 %reduce-scatter.16.cloned.1.call-start = ((), (), s32[]{:S(2)}) async-start(), calls=%async_computation.14 | async-start | bytes 417792 | tf_op jit(solution)/shard_map/reduce_scatter | solution.py:99
  517.8 0.7 copy-start.3
  518.6 171.6 %all-reduce.8.cloned.1.call-start = ((), (), s32[]{:S(2)}) async-start(), calls=%async_computation.15 | async-start | bytes 262144 | tf_op jit(solution)/shard_map/psum | solution.py:105
  632.1 160.2 %reduce-scatter.18.cloned.1.call-start = ((), (), s32[]{:S(2)}) async-start(), calls=%async_computation.16 | async-start | bytes 417792 | tf_op jit(solution)/shard_map/reduce_scatter | solution.py:99
  720.8 0.7 copy-start.4
  721.5 274.2 %reduce-scatter.20.cloned.1.call-start = ((), (), s32[]{:S(2)}) async-start(), calls=%async_computation.17 | async-start | bytes 417792 | tf_op jit(solution)/shard_map/reduce_scatter | solution.py:99
  925.9 0.7 copy-start.5
  926.7 171.5 %all-reduce.10.cloned.1.call-start = ((), (), s32[]{:S(2)}) async-start(), calls=%async_computation.18 | async-start | bytes 262144 | tf_op jit(solution)/shard_map/psum | solution.py:105
  1040.1 160.2 %reduce-scatter.22.cloned.1.call-start = ((), (), s32[]{:S(2)}) async-start(), calls=%async_computation.19 | async-start | bytes 417792 | tf_op jit(solution)/shard_map/reduce_scatter | solution.py:99
  1128.7 0.7 copy-start.6
  1129.5 274.1 %reduce-scatter.24.cloned.1.call-start = ((), (), s32[]{:S(2)}) async-start(), calls=%async_computation.20 | async-start | bytes 417792 | tf_op jit(solution)/shard_map/reduce_scatter | solution.py:99
  1333.8 0.7 copy-start.7
  1334.5 171.6 %all-reduce.12.cloned.1.call-start = ((), (), s32[]{:S(2)}) async-start(), calls=%async_computation.21 | async-start | bytes 262144 | tf_op jit(solution)/shard_map/psum | solution.py:105
  1448.0 160.2 %reduce-scatter.26.cloned.1.call-start = ((), (), s32[]{:S(2)}) async-start(), calls=%async_computation.22 | async-start | bytes 417792 | tf_op jit(solution)/shard_map/reduce_scatter | solution.py:99
  1536.7 0.7 copy-start.8
  1537.4 274.2 %reduce-scatter.28.cloned.1.call-start = ((), (), s32[]{:S(2)}) async-start(), calls=%async_computation.23 | async-start | bytes 417792 | tf_op jit(solution)/shard_map/reduce_scatter | solution.py:99
  1741.8 0.7 copy-start.9
  1742.6 171.6 %all-reduce.14.cloned.1.call-start = ((), (), s32[]{:S(2)}) async-start(), calls=%async_computation.24 | async-start | bytes 262144 | tf_op jit(solution)/shard_map/psum | solution.py:105
  1856.1 160.2 %reduce-scatter.30.cloned.1.call-start = ((), (), s32[]{:S(2)}) async-start(), calls=%async_computation.25 | async-start | bytes 417792 | tf_op jit(solution)/shard_map/reduce_scatter | solution.py:99
  1944.7 0.7 copy-start.10
  1945.5 274.0 %reduce-scatter.32.cloned.1.call-start = ((), (), s32[]{:S(2)}) async-start(), calls=%async_computation.26 | async-start | bytes 417792 | tf_op jit(solution)/shard_map/reduce_scatter | solution.py:99
  2120.6 0.9 copy-start.13
  2149.6 0.7 copy-start
Sparse Core Ops, SparseCore 0:
  105.5 74.0 reduce-scatter.11
  224.3 57.9 all-reduce.5
  313.9 70.6 reduce-scatter.13
  518.7 68.8 reduce-scatter.15
  632.2 57.8 all-reduce.7
  721.7 70.6 reduce-scatter.17
  926.8 68.8 reduce-scatter.19
  1040.3 57.8 all-reduce.9
  1129.6 70.6 reduce-scatter.21
  1334.7 68.8 reduce-scatter.23
  1448.2 57.8 all-reduce.11
  1537.6 70.6 reduce-scatter.25
  1742.7 68.9 reduce-scatter.27
  1856.2 57.9 all-reduce.13
  1945.6 70.6 reduce-scatter.29
  2150.5 68.8 reduce-scatter.31
where the time goes:
time: 2240 us; the launch traced here: 2230 us
  waiting for transfers between devices  1060 us (47%)
  blocking collectives  625 us (28%)
  matrix products  275 us (12%)
  local copies, waits for them, and re-layouts  207 us (9%)
  other arithmetic  30.5 us (1%)
  between operations  22.5 us (1%)
    reduce_scatter x11, waiting for transfers between devices, collect(): lax.psum_scatter(partial_value, 'fas', scatter_dimension=1, tiled=True)  773 us
    psum x5, blocking collectives, local(): image_sq = lax.psum(image_local, ('vox', 'fas'))  314 us
    psum x5, waiting for transfers between devices, local(): lax.psum(backward_partial(whole_rows.reshape(vox_rows, BV, DIRS)), 'vox')  290 us
    psum x5, blocking collectives, local(): grad_sq = lax.psum(jnp.sum(projected * projected), 'fas')  194 us
    dot_general x11, matrix products, forward_accumulate(): jnp.einsum('kvj,kjd->kvd', scaled, atom_blk.astype(jnp.float32), precisio...  124 us
    all_gather x5, blocking collectives, local(): whole_rows = lax.all_gather(residual, 'fas', axis=1, tiled=True)  118 us
    dot_general x11, local copies, waits for them, and re-layouts, forward_accumulate(): jnp.einsum('kvj,kjd->kvd', scaled, atom_blk.astype(jnp.float32), precisio...  94.4 us
    dot_general x11, matrix products, forward_accumulate(): jnp.dot(selector.T, image_blk.reshape(group_size, row_width), precision=l...  81.8 us
  transfers between devices with their start and end apart: 16, of which 16 were waited for; matrix products, arithmetic and copies ran while one was open for 0% of the time, Pallas kernels for 0%

commit v1 on v0

v1 whole, which is shorter than its diff:
```python
import jax
import jax.numpy as jnp
from jax import lax
from jax.experimental import pallas as pl
from jax.experimental.pallas import tpu as pltpu
from jax.sharding import PartitionSpec as P

BV = 64
BF = 64
DIRS = 96
ATOMS = 360
ITERS = 5
SLOTS = 256
ROWS = 16
COLS = 512
NV = 8
NF = 16
QUAD = 4
GROUPS = (SLOTS + (QUAD - 1) * ROWS) // QUAD
GPAD = 80
SPAD = 384
ATOMPAD = 384
HALF = DIRS // 2

f32 = jnp.float32
bf16 = jnp.bfloat16


def low_lanes(shape):
    return lax.broadcasted_iota(jnp.int32, shape, len(shape) - 1) < 64


def split_pair(x):
    h = x.astype(bf16).astype(f32)
    low = x - h
    mask = low_lanes(x.shape)
    first = jnp.where(mask, h, pltpu.roll(low, 64, 1))
    second = jnp.where(mask, pltpu.roll(h, 64, 1), low)
    return first.astype(bf16), second.astype(bf16)


def fold(x):
    return x + pltpu.roll(x, 64, 1)


def kernel(
    perm,
    grow,
    last,
    valid,
    keep,
    has,
    coef,
    atoms,
    dict_t,
    cols_lane,
    cols_sub,
    w_in,
    sig_in,
    w_out,
    res_out,
    cg,
    at,
    sel,
    sel_t,
    u_p,
    u_w,
    buf,
    part,
    rs_in,
    r_all,
    r_two,
    contrib,
    b_two,
    g_part,
    g_in,
    g_all,
    p_two,
    sc_f,
    sc_v,
    sg_in,
    turn,
    sig_own,
    fin_out,
    fin_in,
    s_sig,
    r_sig,
    s_rs,
    r_rs,
    s_ag,
    r_ag,
    s_gr,
    r_gr,
    s_ga,
    r_ga,
    s_sf,
    r_sf,
    s_sv,
    r_sv,
    s_fin,
    r_fin,
):
    me_v = lax.axis_index("vox")
    me_f = lax.axis_index("fas")

    def copies(axis, src_at, dst, send_sem, recv_sem):
        n, me = (NF, me_f) if axis == "fas" else (NV, me_v)
        out, arrive = [], []
        for off in range(1, n):
            peer = lax.rem(me + off, n)
            out.append(
                pltpu.make_async_remote_copy(
                    src_ref=src_at(peer),
                    dst_ref=dst.at[me],
                    send_sem=send_sem.at[peer],
                    recv_sem=recv_sem.at[me],
                    device_id={axis: peer},
                    device_id_type=pl.DeviceIdType.MESH,
                )
            )
            arrive.append(
                pltpu.make_async_remote_copy(
                    src_ref=src_at(peer),
                    dst_ref=dst.at[peer],
                    send_sem=send_sem.at[peer],
                    recv_sem=recv_sem.at[peer],
                    device_id={axis: peer},
                    device_id_type=pl.DeviceIdType.MESH,
                )
            )

        def start():
            for c in out:
                c.start()

        def wait():
            for c in arrive:
                c.wait_recv()
            for c in out:
                c.wait_send()

        return start, wait

    barrier = pltpu.get_barrier_semaphore()
    for axis, n, me in (("fas", NF, me_f), ("vox", NV, me_v)):
        for off in range(1, n):
            pl.semaphore_signal(
                barrier,
                inc=1,
                device_id={axis: lax.rem(me + off, n)},
                device_id_type=pl.DeviceIdType.MESH,
            )

    def build(g, carry):
        mask = low_lanes((BV, 128))
        for half in range(2):
            k0 = g * QUAD + 2 * half
            x = coef[perm[k0]].astype(f32) * valid[k0]
            y = coef[perm[k0 + 1]].astype(f32) * valid[k0 + 1]
            cg[g, :, half * 128 : (half + 1) * 128] = jnp.where(mask, x, y).astype(bf16)
        row = atoms[pl.ds(g, 1), :]
        hot = (lax.broadcasted_iota(jnp.int32, (ATOMPAD, 256), 0) == row).astype(f32).astype(bf16)
        at[g] = jnp.dot(dict_t[...], hot, preferred_element_type=f32).astype(bf16)
        return carry

    lax.fori_loop(0, GROUPS, build, 0)
    sel[...] = (
        (lax.broadcasted_iota(jnp.int32, (COLS, SPAD), 0) == cols_lane[...]).astype(f32).astype(bf16)
    )
    sel_t[...] = (
        (lax.broadcasted_iota(jnp.int32, (SPAD, COLS), 1) == cols_sub[...]).astype(f32).astype(bf16)
    )
    contrib[...] = jnp.zeros_like(contrib)
    b_two[...] = jnp.zeros_like(b_two)

    pl.semaphore_wait(barrier, NF - 1 + NV - 1)

    start_sig, wait_sig = copies("fas", lambda p: sig_in.at[p // 2], sg_in, s_sig, r_sig)
    start_sig()

    def gather(values, u_ref):
        first, second = split_pair(values)
        p_two[0:256, :] = first
        p_two[256:512, :] = second
        got = fold(jnp.dot(sel_t[...], p_two[...], preferred_element_type=f32))
        mask = low_lanes((GPAD, 128))
        u_ref[:, 0:128] = jnp.where(mask, got[0:GPAD], got[GPAD : 2 * GPAD])
        u_ref[:, 128:256] = jnp.where(mask, got[2 * GPAD : 3 * GPAD], got[3 * GPAD : 4 * GPAD])

    def forward(u_ref):
        def step(g, acc):
            scaled = cg[g].astype(f32) * u_ref[pl.ds(g, 1), :]
            high = scaled.astype(bf16)
            low = (scaled - high.astype(f32)).astype(bf16)
            both = jnp.concatenate([high, low], axis=0)
            made = lax.dot_general(
                at[g], both, (((1,), (1,)), ((), ())), preferred_element_type=f32
            )
            acc = acc * keep[g] + made
            buf[g] = acc
            return acc

        lax.fori_loop(0, GROUPS, step, jnp.zeros((DIRS, 128), f32), unroll=4)
        mask = low_lanes((DIRS, 128))
        for pair in range(ROWS // 2):
            even = fold(buf[last[2 * pair]] * has[2 * pair])
            odd = fold(buf[last[2 * pair + 1]] * has[2 * pair + 1])
            both = jnp.where(mask, even, odd)
            part[2 * pair] = both[:HALF]
            part[2 * pair + 1] = both[HALF:]

    start_rs, wait_rs = copies("fas", lambda p: part.at[p], rs_in, s_rs, r_rs)
    start_ag, wait_ag = copies("fas", lambda p: r_all.at[me_f], r_all, s_ag, r_ag)
    start_gr, wait_gr = copies("vox", lambda p: g_part.at[p], g_in, s_gr, r_gr)
    start_ga, wait_ga = copies("vox", lambda p: g_all.at[me_v], g_all, s_ga, r_ga)
    start_sf, wait_sf = copies("fas", lambda p: sc_f.at[me_f], sc_f, s_sf, r_sf)
    start_sv, wait_sv = copies("vox", lambda p: sc_v.at[me_v], sc_v, s_sv, r_sv)
    start_fin, wait_fin = copies("fas", lambda p: fin_out.at[p], fin_in, s_fin, r_fin)

    def reduce_fas():
        start_rs()
        wait_rs()
        total = part[me_f]
        for off in range(1, NF):
            total = total + rs_in[lax.rem(me_f + off, NF)]
        return total

    w_out[...] = w_in[...]
    gather(w_in[...], u_w)
    forward(u_w)
    start_rs()
    wait_sig()
    sg_in[me_f] = sig_in[me_f // 2]
    for f in range(NF):
        for r in range(2):
            turn[r * 64 + f * 4 : r * 64 + f * 4 + 4, :] = sg_in[f, r * 4 : r * 4 + 4, :]
    turn[...] = jnp.transpose(turn[...])
    half_at = pl.multiple_of(lax.rem(me_f, 2) * HALF, 8)
    sig_own[...] = turn[pl.ds(half_at, HALF), :]
    wait_rs()
    total = part[me_f]
    for off in range(1, NF):
        total = total + rs_in[lax.rem(me_f + off, NF)]
    r_all[me_f] = total - sig_own[...]

    def sweep(_, carry):
        start_ag()
        wait_ag()
        for pair in range(ROWS // 2):
            x = jnp.concatenate([r_all[2 * pair], r_all[2 * pair + 1]], axis=0)
            even, odd = split_pair(x)
            r_two[2 * pair] = even
            r_two[2 * pair + 1] = odd

        def step(g, c):
            block = cg[g]
            twice = jnp.concatenate([block, block], axis=0)
            inner = jnp.dot(r_two[grow[g]], twice, preferred_element_type=f32)
            contrib[pl.ds(g, 1), :] = jnp.sum(inner * at[g].astype(f32), axis=0, keepdims=True)
            return c

        lax.fori_loop(0, GROUPS, step, 0, unroll=4)
        for half in range(2):
            first, second = split_pair(contrib[:, half * 128 : (half + 1) * 128])
            b_two[2 * half * GPAD : (2 * half + 1) * GPAD, :] = first
            b_two[(2 * half + 1) * GPAD : (2 * half + 2) * GPAD, :] = second
        got = fold(jnp.dot(sel[...], b_two[...], preferred_element_type=f32))
        mask = low_lanes((256, 128))
        g_part[...] = jnp.where(mask, got[0:256], got[256:512]).reshape(NV, 32, 128)
        start_gr()
        wait_gr()
        total = g_part[me_v]
        for off in range(1, NV):
            total = total + g_in[lax.rem(me_v + off, NV)]
        g_all[me_v] = total
        start_ga()
        wait_ga()
        weights = w_out[...]
        gradient = g_all[...].reshape(256, 128)
        projected = jnp.where((weights > 0) | (gradient < 0), gradient, 0.0)
        gather(projected, u_p)
        forward(u_p)
        image = reduce_fas()
        sc_f[me_f, 0:8] = jnp.sum((projected * projected).reshape(32, 8, 128), axis=0)
        sc_f[me_f, 8:16] = jnp.sum((image * image).reshape(6, 8, 128), axis=0)
        start_sf()
        wait_sf()
        sums = sc_f[0]
        for f in range(1, NF):
            sums = sums + sc_f[f]
        sc_v[me_v] = sums[8:16]
        start_sv()
        wait_sv()
        squares = sc_v[0]
        for v in range(1, NV):
            squares = squares + sc_v[v]
        grad_sq = jnp.sum(sums[0:8], axis=(0, 1), keepdims=True)
        image_sq = jnp.sum(squares, axis=(0, 1), keepdims=True)
        size = grad_sq / (image_sq + 1e-06)
        w_out[...] = jnp.maximum(weights - size * projected, 0.0)
        u_w[...] = jnp.maximum(u_w[...] - size * u_p[...], 0.0)
        forward(u_w)
        r_all[me_f] = reduce_fas() - sig_own[...]
        return carry

    lax.fori_loop(0, ITERS, sweep, 0)

    turn[0:HALF, :] = r_all[me_f]
    turn[HALF:, :] = jnp.zeros((128 - HALF, 128), f32)
    turn[...] = jnp.transpose(turn[...])
    for f in range(NF):
        for r in range(2):
            fin_out[f, r * 4 : r * 4 + 4, :] = turn[r * 64 + f * 4 : r * 64 + f * 4 + 4, :]
    start_fin()
    wait_fin()
    fin_in[me_f] = fin_out[me_f]
    res_out[...] = fin_in[...]


def local(
    signal,
    initial_weights,
    coefficients,
    block_rows,
    block_cols,
    block_atoms,
    block_count,
    dictionary,
):
    i32 = jnp.int32
    rows = block_rows - lax.axis_index("vox") * ROWS
    cols = block_cols - lax.axis_index("fas") * COLS
    slots = jnp.arange(SLOTS, dtype=i32)
    lives = slots < block_count[0]
    hot = (rows[:, None] == jnp.arange(ROWS, dtype=i32)[None, :]) & lives[:, None]
    before = (slots[None, :] < slots[:, None]) & lives[None, :] & (rows[None, :] == rows[:, None])
    rank = jnp.sum(before.astype(i32), axis=1)
    count = jnp.sum(hot.astype(i32), axis=0)
    groups = (count + QUAD - 1) // QUAD
    span = jnp.arange(ROWS, dtype=i32)
    ends = jnp.sum(jnp.where(span[None, :] <= span[:, None], groups[None, :], 0), axis=1)
    firsts = ends - groups
    place = jnp.where(
        lives, jnp.sum(jnp.where(hot, firsts[None, :], 0), axis=1) * QUAD + rank, -1
    )
    spots = jnp.arange(GPAD * QUAD, dtype=i32)
    match = place[None, :] == spots[:, None]
    perm = jnp.sum(jnp.where(match, slots[None, :], 0), axis=1)
    filled = jnp.any(match, axis=1)
    col_at = jnp.sum(jnp.where(match, cols[None, :] + 1, 0), axis=1) - 1
    col_q = jnp.concatenate(
        [col_at.reshape(GPAD, QUAD).T.reshape(-1), jnp.full((SPAD - GPAD * QUAD,), -1, i32)]
    )
    turns = jnp.arange(GPAD, dtype=i32)
    grow = jnp.minimum(jnp.sum((ends[None, :] <= turns[:, None]).astype(i32), axis=1), ROWS - 1)
    is_first = jnp.any((firsts[None, :] == turns[:, None]) & (groups[None, :] > 0), axis=1)
    keep = 1.0 - is_first.astype(f32)
    last = jnp.maximum(ends - 1, 0)
    has = (groups > 0).astype(f32)
    atoms = block_atoms[perm].reshape(GPAD, QUAD * BF)
    coef = coefficients.reshape(SLOTS, BV, BF)
    coef = jnp.concatenate([coef, coef], axis=2)
    dict_t = jnp.pad(dictionary.T, ((0, 0), (0, ATOMPAD - ATOMS)))
    w_in = initial_weights.reshape(2, 256, BF)
    w_in = jnp.concatenate([w_in[0], w_in[1]], axis=1)
    sig_in = jnp.pad(signal.reshape(8, 8, DIRS), ((0, 0), (0, 0), (0, 128 - DIRS)))

    smem = pl.BlockSpec(memory_space=pltpu.SMEM)
    vmem = pl.BlockSpec(memory_space=pltpu.VMEM)
    dma = pltpu.SemaphoreType.DMA
    w_new, res = pl.pallas_call(
        kernel,
        out_shape=(
            jax.ShapeDtypeStruct((256, 128), f32),
            jax.ShapeDtypeStruct((NF, 8, 128), f32),
        ),
        in_specs=[smem] * 6 + [vmem] * 7,
        out_specs=(vmem, vmem),
        scratch_shapes=[
            pltpu.VMEM((GROUPS, BV, 256), bf16),
            pltpu.VMEM((GROUPS, DIRS, 256), bf16),
            pltpu.VMEM((COLS, SPAD), bf16),
            pltpu.VMEM((SPAD, COLS), bf16),
            pltpu.VMEM((GPAD, 256), f32),
            pltpu.VMEM((GPAD, 256), f32),
            pltpu.VMEM((GROUPS, DIRS, 128), f32),
            pltpu.VMEM((NF, HALF, 128), f32),
            pltpu.VMEM((NF, HALF, 128), f32),
            pltpu.VMEM((NF, HALF, 128), f32),
            pltpu.VMEM((ROWS, DIRS, 128), bf16),
            pltpu.VMEM((GPAD, 256), f32),
            pltpu.VMEM((SPAD, 128), bf16),
            pltpu.VMEM((NV, 32, 128), f32),
            pltpu.VMEM((NV, 32, 128), f32),
            pltpu.VMEM((NV, 32, 128), f32),
            pltpu.VMEM((COLS, 128), bf16),
            pltpu.VMEM((NF, 16, 128), f32),
            pltpu.VMEM((NV, 8, 128), f32),
            pltpu.VMEM((NF, 8, 128), f32),
            pltpu.VMEM((128, 128), f32),
            pltpu.VMEM((HALF, 128), f32),
            pltpu.VMEM((NF, 8, 128), f32),
            pltpu.VMEM((NF, 8, 128), f32),
        ]
        + [dma((NF,)), dma((NF,))] * 3
        + [dma((NV,)), dma((NV,))] * 2
        + [dma((NF,)), dma((NF,)), dma((NV,)), dma((NV,)), dma((NF,)), dma((NF,))],
        compiler_params=pltpu.CompilerParams(
            collective_id=0, has_side_effects=True, vmem_limit_bytes=48 * 1024 * 1024
        ),
    )(
        perm,
        grow,
        last,
        filled.astype(f32),
        keep,
        has,
        coef,
        atoms,
        dict_t,
        col_q[None, :],
        col_q[:, None],
        w_in,
        sig_in,
    )
    weights = jnp.concatenate([w_new[:, :BF], w_new[:, BF:]], axis=0).reshape(-1)
    res = res[:, :, :HALF].reshape(8, 2, 8, HALF).transpose(0, 2, 1, 3)
    return (weights, res.reshape(ROWS, 4 * DIRS))


def solution(mesh):
    placed = (
        P("vox", "fas"),
        P("fas"),
        P(("vox", "fas"), None),
        P(("vox", "fas")),
        P(("vox", "fas")),
        P(("vox", "fas"), None),
        P(("vox", "fas")),
        P(),
    )
    return jax.shard_map(
        local, mesh=mesh, in_specs=placed, out_specs=(P("fas"), P("vox", "fas")), check_vma=False
    )
```

time: 2240 us -> 333 us (0.15)
  waiting for transfers between devices: 1060 us -> 0 us
  blocking collectives: 625 us -> 0 us
  Pallas kernels: 0 us -> 306 us
  matrix products: 275 us -> 0 us
  local copies, waits for them, and re-layouts: 207 us -> 15.7 us
    reduce_scatter x11 -> x0, waiting for transfers between devices: 773 us -> none  [collect(): lax.psum_scatter(partial_value, 'fas', scatter_dimension=1, tiled=True)]
    psum x10 -> x0, blocking collectives: 507 us -> none  [the longest x5 314 us: local(): image_sq = lax.psum(image_local, ('vox', 'fas'))]
    pallas_call x0 -> x1, Pallas kernels: none -> 306 us  [local(): pl.pallas_call(kernel, out_shape=(jax.ShapeDtypeStruct((256, 128), f32),...]
    psum x5 -> x0, waiting for transfers between devices: 290 us -> none  [local(): lax.psum(backward_partial(whole_rows.reshape(vox_rows, BV, DIRS)), 'vox')]
    dot_general x32 -> x0, matrix products: 275 us -> none  [the longest x11 124 us: forward_accumulate(): jnp.einsum('kvj,kjd->kvd', scaled, atom_blk.astype(jnp.float32), precisio...]
    all_gather x5 -> x0, blocking collectives: 118 us -> none  [local(): whole_rows = lax.all_gather(residual, 'fas', axis=1, tiled=True)]
    dot_general x11 -> x0, local copies, waits for them, and re-layouts: 94.4 us -> none  [forward_accumulate(): jnp.einsum('kvj,kjd->kvd', scaled, atom_blk.astype(jnp.float32), precisio...]
    gather x17 -> x1, local copies, waits for them, and re-layouts: 87.2 us -> 1.08 us  [local(): atoms = block_atoms[perm].reshape(GPAD, QUAD * BF)]
  transfers between devices with their start and end apart: 16 -> 0, of which waited for: 16 -> 0; matrix products, arithmetic and copies ran while one was open for 0% -> 0% of each run, Pallas kernels for 0% -> 0%
where the time goes in v1:
time: 333 us
  Pallas kernels  306 us (92%)
  local copies, waits for them, and re-layouts  15.7 us (5%)
  other arithmetic  9.65 us (3%)
    pallas_call x1, Pallas kernels, local(): pl.pallas_call(kernel, out_shape=(jax.ShapeDtypeStruct((256, 128), f32),...  306 us
    concatenate x1, other arithmetic, local(): coef = jnp.concatenate([coef, coef], axis=2)  7.04 us
    reshape x1, local copies, waits for them, and re-layouts, local(): coef = coefficients.reshape(SLOTS, BV, BF)  6.69 us

profile of v1, /device:TPU:0, one launch (start us, length us, event | category | flops | bytes accessed | tf_op | source)
XLA Modules:
  0.0 333.2 jit_solution(11375921032752212332)
XLA Ops:
  0.6 0.7 broadcast_subtract_fusion
  2.0 0.2 convert_reduce_fusion
  2.2 0.1 convert_reduce_fusion.1
  2.3 0.1 select_reduce_fusion.3
  2.4 0.1 select_reduce_fusion.2
  2.5 0.7 subtract_add_fusion
  3.2 0.2 select_reduce_fusion
  3.4 0.1 convert_reduce_fusion.2
  3.5 0.1 fusion
  3.7 0.1 fusion.5
  3.8 3.3 copy.19
  7.0 6.7 %copy.20 = bf16[256,64,64]{2,1,0:T(8,128)(2,1)} copy(bf16[256,64,64]{0,2,1:T(8,128)(2,1)S(1)} %bitcast.11) | data formatting | bytes 4194304 | tf_op jit(solution)/shard_map/reshape | solution.py:361
  13.7 0.0 copy-start.3
  13.7 0.0 copy-start.2
  13.7 0.0 copy-start.1
  13.8 0.0 copy-start.4
  13.8 7.0 %pad_maximum_fusion.coef = bf16[256,64,128]{2,1,0:T(8,128)(2,1)} fusion(bf16[256,64,64]{2,1,0:T(8,128)(2,1)} %copy.20), kind=kLoop, calls=%fused_computation.1 | loop fusion | flops 8388608 | bytes 6291456 | tf_op jit(solution)/shard_map/concatenate | solution.py:362
  20.8 0.0 copy-done.3
  20.8 0.1 copy.22
  20.9 1.1 gather_fusion
  22.0 0.1 reshape.113.atoms
  22.1 0.0 copy-done.2
  22.2 0.1 sub.55
  22.3 0.1 copy.23
  22.3 0.1 reshape.114
  22.4 0.1 broadcast_in_dim.85.cols_sub
  22.6 0.0 copy-done.1
  22.6 0.1 slice.40
  22.7 0.1 slice.38
  22.8 0.1 pad_maximum_fusion.2.w_in
  22.9 0.0 copy-done.4
  22.9 0.1 reshape.115
  23.0 0.0 copy-start
  23.0 2.2 copy-done
  25.2 306.4 %shard_map.95 = (f32[256,128]{1,0:T(8,128)S(1)}, f32[16,8,128]{2,1,0:T(8,128)S(1)}) custom-call(s32[320]{0:T(512)S(1)} %get-tuple-element.7.perm, s32[80]{0:T(128)S(1)} %broadcast_minimum_fusion.grow, s32[16]{0:T(128)S(1)} %get-tuple-element.14.last, f32[320]{0:T(512)S(1)} %convert_element_type.25.valid, f32[80]{0:T(128)S(1)} %convert_subtract_fusion.keep, ...), custom_call_target="tpu_custom_call" | custom-call | tf_op jit(solution)/shard_map/pallas_call | solution.py:371
  331.5 0.1 fusion.8
  331.7 0.8 reshape.116
  332.5 0.7 reshape.118
  (17 shorter events, 0.2 us)
Async XLA Ops:
  13.7 7.1 %copy-start.3 = (s32[256,64]{0,1:T(8,128)S(1)}, s32[256,64]{0,1:T(8,128)}, u32[]{:S(2)}) copy-start(s32[256,64]{0,1:T(8,128)} %param.13) | copy-start | bytes 196612
  13.7 8.4 %copy-start.2 = (bf16[360,96]{0,1:T(8,128)(2,1)S(1)}, bf16[360,96]{0,1:T(8,128)(2,1)}, u32[]{:S(2)}) copy-start(bf16[360,96]{0,1:T(8,128)(2,1)} %param.15) | copy-start | bytes 207364
  13.7 8.8 %copy-start.1 = (f32[32768]{0:T(1024)S(1)}, f32[32768]{0:T(1024)}, u32[]{:S(2)}) copy-start(f32[32768]{0:T(1024)} %param.9) | copy-start | bytes 393220
  13.8 9.1 %copy-start.4 = (f32[16,384]{1,0:T(8,128)S(1)}, f32[16,384]{1,0:T(8,128)}, u32[]{:S(2)}) copy-start(f32[16,384]{1,0:T(8,128)} %param.8) | copy-start | bytes 73732
  23.0 2.2 copy-start

commit v2 on v1

v2 whole, which is shorter than its diff:
```python
import jax
import jax.numpy as jnp
from jax import lax
from jax.experimental import pallas as pl
from jax.experimental.pallas import tpu as pltpu
from jax.sharding import PartitionSpec as P

BV = 64
BF = 64
DIRS = 96
ATOMS = 360
ITERS = 5
SLOTS = 256
ROWS = 16
COLS = 512
NV = 8
NF = 16
SIDE = 4
CHIPS = 64
QUAD = 4
GROUPS = (SLOTS + (QUAD - 1) * ROWS) // QUAD
GPAD = 80
SPAD = 384
ATOMPAD = 384
HALF = DIRS // 2


def hops(off):
    return sum(min(d, SIDE - d) for d in off)


CHIP_FAR_FIRST = sorted(
    [(y, z, x) for y in range(SIDE) for z in range(SIDE) for x in range(SIDE) if y + z + x],
    key=lambda off: (-hops(off), off),
)
FAR_FIRST = [off[1:] for off in CHIP_FAR_FIRST if off[0] == 0]

f32 = jnp.float32
bf16 = jnp.bfloat16


def low_lanes(shape):
    return lax.broadcasted_iota(jnp.int32, shape, len(shape) - 1) < 64


def split_pair(x):
    h = x.astype(bf16).astype(f32)
    low = x - h
    mask = low_lanes(x.shape)
    first = jnp.where(mask, h, pltpu.roll(low, 64, 1))
    second = jnp.where(mask, pltpu.roll(h, 64, 1), low)
    return first.astype(bf16), second.astype(bf16)


def fold(x):
    return x + pltpu.roll(x, 64, 1)


def kernel(
    grow,
    last,
    keep,
    has,
    coef_hbm,
    digits,
    dict_t,
    place_lane,
    cols_lane,
    cols_sub,
    w_in,
    sig_in,
    w_out,
    res_out,
    coef,
    wide,
    pick,
    names,
    cg,
    at,
    sel,
    sel_t,
    u_p,
    u_w,
    buf,
    part,
    rs_in,
    r_all,
    r_two,
    contrib,
    b_two,
    g_part,
    g_pair,
    g_in,
    g_all,
    p_two,
    sc_in,
    sc_pair,
    sg_in,
    turn,
    sig_own,
    fin_out,
    fin_in,
    s_sig,
    r_sig,
    s_rs,
    r_rs,
    s_ag,
    r_ag,
    s_gr,
    r_gr,
    s_sc,
    r_sc,
    s_fin,
    r_fin,
    s_two,
    r_twin,
    s_coef,
):
    me_v = lax.axis_index("vox")
    me_f = lax.axis_index("fas")
    me_c = lax.rem(me_v, 2)
    me_y = me_v // 2
    twin = me_v + 1 - 2 * me_c
    fetch = pltpu.make_async_copy(coef_hbm, coef, s_coef)
    fetch.start()

    def remote(src, dst, send_sem, recv_sem, device):
        return pltpu.make_async_remote_copy(
            src_ref=src,
            dst_ref=dst,
            send_sem=send_sem,
            recv_sem=recv_sem,
            device_id=device,
            device_id_type=pl.DeviceIdType.MESH,
        )

    def pair(out, arrive):
        def start():
            for c in out:
                c.start()

        def wait():
            for c in arrive:
                c.wait_recv()
            for c in out:
                c.wait_send()

        return start, wait

    def copies(src_at, dst, send_sem, recv_sem):
        out, arrive = [], []
        for off in FAR_FIRST:
            peer = other_fas(off)
            where = {"fas": peer}
            out.append(
                remote(src_at(peer), dst.at[me_f], send_sem.at[peer], recv_sem.at[me_f], where)
            )
            arrive.append(
                remote(src_at(peer), dst.at[peer], send_sem.at[peer], recv_sem.at[peer], where)
            )
        return pair(out, arrive)

    def other_fas(off):
        return lax.rem(me_f // SIDE + off[0], SIDE) * SIDE + lax.rem(me_f + off[1], SIDE)

    def with_twin(src, dst, landing, index):
        sems, where = (s_two.at[index], r_twin.at[index]), {"vox": twin}
        return pair([remote(src, dst, *sems, where)], [remote(src, landing, *sems, where)])

    barrier = pltpu.get_barrier_semaphore()
    pl.semaphore_signal(
        barrier, inc=1, device_id={"vox": twin}, device_id_type=pl.DeviceIdType.MESH
    )
    for off in CHIP_FAR_FIRST:
        pl.semaphore_signal(
            barrier,
            inc=1,
            device_id={"vox": lax.rem(me_y + off[0], SIDE) * 2 + me_c, "fas": other_fas(off[1:])},
            device_id_type=pl.DeviceIdType.MESH,
        )

    turn_row = lax.broadcasted_iota(jnp.int32, (GPAD, SLOTS), 0) * QUAD
    for q in range(QUAD):
        hot = (place_lane[...] == turn_row + q).astype(f32).astype(bf16)
        pick[q * GPAD : (q + 1) * GPAD, :] = hot
    pick[QUAD * GPAD :, :] = jnp.zeros((SPAD - QUAD * GPAD, SLOTS), bf16)
    found = jnp.dot(pick[0 : QUAD * GPAD, :], digits[...], preferred_element_type=f32)
    found = jnp.where(low_lanes(found.shape), found, found * 256.0)
    found = fold(found)
    mask = low_lanes((GPAD, 128))
    names[:, 0:128] = jnp.where(mask, found[0:GPAD], found[GPAD : 2 * GPAD])
    names[:, 128:256] = jnp.where(mask, found[2 * GPAD : 3 * GPAD], found[3 * GPAD :])

    def name_atoms(g, carry):
        row = names[pl.ds(g, 1), :].astype(jnp.int32)
        hot = (lax.broadcasted_iota(jnp.int32, (ATOMPAD, 256), 0) == row).astype(f32).astype(bf16)
        at[g] = jnp.dot(dict_t[...], hot, preferred_element_type=f32).astype(bf16)
        return carry

    lax.fori_loop(0, GROUPS, name_atoms, 0, unroll=4)
    where_col = (lax.broadcasted_iota(jnp.int32, (COLS, SLOTS), 0) == cols_lane[...]).astype(f32)
    sel[...] = lax.dot_general(
        where_col.astype(bf16), pick[...], (((1,), (1,)), ((), ())), preferred_element_type=f32
    ).astype(bf16)
    where_col = (lax.broadcasted_iota(jnp.int32, (SLOTS, COLS), 1) == cols_sub[...]).astype(f32)
    sel_t[...] = jnp.dot(
        pick[...], where_col.astype(bf16), preferred_element_type=f32
    ).astype(bf16)
    contrib[...] = jnp.zeros_like(contrib)
    b_two[...] = jnp.zeros_like(b_two)

    pl.semaphore_wait(barrier, CHIPS)
    start_sig, wait_sig = copies(lambda p: sig_in.at[p // 2], sg_in, s_sig, r_sig)
    start_sig()

    fetch.wait()

    def spread(t, carry):
        at_lane = pl.multiple_of(t * 128, 128)
        moved = jnp.dot(pick[0 : QUAD * GPAD, :], coef[:, pl.ds(at_lane, 128)], preferred_element_type=f32)
        mask = low_lanes((GPAD, 128))
        for half in range(2):
            x = moved[2 * half * GPAD : (2 * half + 1) * GPAD]
            y = moved[(2 * half + 1) * GPAD : (2 * half + 2) * GPAD]
            lanes = slice(half * 128, half * 128 + 128)
            even = jnp.where(mask, x, pltpu.roll(y, 64, 1))
            odd = jnp.where(mask, pltpu.roll(x, 64, 1), y)
            first = pl.multiple_of(t * (2 * GPAD), 8)
            wide[half, pl.ds(first, GPAD), :] = even
            wide[half, pl.ds(first + GPAD, GPAD), :] = odd
        return carry

    lax.fori_loop(0, BV // 2, spread, 0, unroll=4)

    def bring(g, carry):
        for half in range(2):
            block = wide[half, pl.ds(g, BV, stride=GPAD), :]
            cg[g, :, half * 128 : half * 128 + 128] = block.astype(bf16)
        return carry

    lax.fori_loop(0, GROUPS, bring, 0, unroll=4)


    def gather(values, u_ref):
        first, second = split_pair(values)
        p_two[0:256, :] = first
        p_two[256:512, :] = second
        got = fold(jnp.dot(sel_t[...], p_two[...], preferred_element_type=f32))
        mask = low_lanes((GPAD, 128))
        u_ref[:, 0:128] = jnp.where(mask, got[0:GPAD], got[GPAD : 2 * GPAD])
        u_ref[:, 128:256] = jnp.where(mask, got[2 * GPAD : 3 * GPAD], got[3 * GPAD : 4 * GPAD])

    def forward(u_ref):
        def step(g, acc):
            scaled = cg[g].astype(f32) * u_ref[pl.ds(g, 1), :]
            high = scaled.astype(bf16)
            low = (scaled - high.astype(f32)).astype(bf16)
            both = jnp.concatenate([high, low], axis=0)
            made = lax.dot_general(
                at[g], both, (((1,), (1,)), ((), ())), preferred_element_type=f32
            )
            acc = acc * keep[g] + made
            buf[g] = acc
            return acc

        lax.fori_loop(0, GROUPS, step, jnp.zeros((DIRS, 128), f32), unroll=19)
        mask = low_lanes((DIRS, 128))
        for pair in range(ROWS // 2):
            even = fold(buf[last[2 * pair]] * has[2 * pair])
            odd = fold(buf[last[2 * pair + 1]] * has[2 * pair + 1])
            both = jnp.where(mask, even, odd)
            part[2 * pair] = both[:HALF]
            part[2 * pair + 1] = both[HALF:]

    start_rs, wait_rs = copies(lambda p: part.at[p], rs_in, s_rs, r_rs)
    start_ag, wait_ag = copies(lambda p: r_all.at[me_f], r_all, s_ag, r_ag)
    start_fin, wait_fin = copies(lambda p: fin_out.at[p], fin_in, s_fin, r_fin)

    start_swap, wait_swap = with_twin(g_part.at[1 - me_c], g_pair, g_pair, 0)
    start_back, wait_back = with_twin(g_all.at[me_c], g_all.at[me_c], g_all.at[1 - me_c], 1)
    out, arrive = [], []
    for off in (2, 1, 3):
        y = lax.rem(me_y + off, SIDE)
        where = {"vox": y * 2 + me_c}
        out.append(remote(g_in.at[me_y], g_in.at[me_y], s_gr.at[y], r_gr.at[me_y], where))
        arrive.append(remote(g_in.at[y], g_in.at[y], s_gr.at[y], r_gr.at[y], where))
    start_gr, wait_gr = pair(out, arrive)

    mine = me_y * NF + me_f
    out, arrive = [], []
    for off in CHIP_FAR_FIRST:
        y, f = lax.rem(me_y + off[0], SIDE), other_fas(off[1:])
        where = {"vox": y * 2 + me_c, "fas": f}
        chip = y * NF + f
        src = sc_in.at[mine, 0:1]
        out.append(remote(src, src, s_sc.at[chip], r_sc.at[mine], where))
        src = sc_in.at[chip, 0:1]
        arrive.append(remote(src, src, s_sc.at[chip], r_sc.at[chip], where))
    start_sc, wait_sc = pair(out, arrive)
    start_two, wait_two = with_twin(sc_pair.at[me_c], sc_pair.at[me_c], sc_pair.at[1 - me_c], 2)

    def added():
        total = part[me_f]
        for off in range(1, NF):
            total = total + rs_in[lax.rem(me_f + off, NF)]
        return total

    def reduce_fas():
        start_rs()
        wait_rs()
        return added()

    w_out[...] = w_in[...]
    gather(w_in[...], u_w)
    forward(u_w)
    start_rs()
    wait_sig()
    sg_in[me_f] = sig_in[me_f // 2]
    for f in range(NF):
        for r in range(2):
            turn[r * 64 + f * 4 : r * 64 + f * 4 + 4, :] = sg_in[f, r * 4 : r * 4 + 4, :]
    turn[...] = jnp.transpose(turn[...])
    half_at = pl.multiple_of(lax.rem(me_f, 2) * HALF, 8)
    sig_own[...] = turn[pl.ds(half_at, HALF), :]
    wait_rs()
    r_all[me_f] = added() - sig_own[...]

    def sweep(_, carry):
        start_ag()
        wait_ag()
        for pair in range(ROWS // 2):
            x = jnp.concatenate([r_all[2 * pair], r_all[2 * pair + 1]], axis=0)
            even, odd = split_pair(x)
            r_two[2 * pair] = even
            r_two[2 * pair + 1] = odd

        def step(g, c):
            block = cg[g]
            twice = jnp.concatenate([block, block], axis=0)
            inner = jnp.dot(r_two[grow[g]], twice, preferred_element_type=f32)
            contrib[pl.ds(g, 1), :] = jnp.sum(inner * at[g].astype(f32), axis=0, keepdims=True)
            return c

        lax.fori_loop(0, GROUPS, step, 0, unroll=19)
        for half in range(2):
            first, second = split_pair(contrib[:, half * 128 : (half + 1) * 128])
            b_two[2 * half * GPAD : (2 * half + 1) * GPAD, :] = first
            b_two[(2 * half + 1) * GPAD : (2 * half + 2) * GPAD, :] = second
        got = fold(jnp.dot(sel[...], b_two[...], preferred_element_type=f32))
        mask = low_lanes((256, 128))
        g_part[...] = jnp.where(mask, got[0:256], got[256:512]).reshape(2, 128, 128)
        start_swap()
        wait_swap()
        g_in[me_y] = g_part[me_c] + g_pair[...]
        start_gr()
        wait_gr()
        g_all[me_c] = (g_in[0] + g_in[1]) + (g_in[2] + g_in[3])
        start_back()
        wait_back()
        weights = w_out[...]
        gradient = g_all[...].reshape(256, 128)
        projected = jnp.where((weights > 0) | (gradient < 0), gradient, 0.0)
        gather(projected, u_p)
        forward(u_p)
        image = reduce_fas()
        squares = jnp.sum((image * image).reshape(6, 8, 128), axis=0)
        steep = jnp.sum((projected * projected).reshape(32, 8, 128), axis=0)
        squares = jnp.sum(fold(squares), axis=0, keepdims=True)
        steep = jnp.sum(fold(steep), axis=0, keepdims=True)
        sc_in[mine, 0:1, :] = jnp.where(low_lanes((1, 128)), squares, steep)
        start_sc()
        wait_sc()
        sums = jnp.sum(sc_in[:, 0, :], axis=0, keepdims=True)
        sc_pair[me_c] = jnp.broadcast_to(sums, (8, 128))
        start_two()
        wait_two()
        both = sc_pair[0, 0:1, :] + sc_pair[1, 0:1, :]
        mask = low_lanes((1, 128))
        image_sq = jnp.sum(jnp.where(mask, both, 0.0), axis=(0, 1), keepdims=True)
        grad_sq = jnp.sum(jnp.where(mask, 0.0, both), axis=(0, 1), keepdims=True) * (1.0 / NV)
        size = grad_sq / (image_sq + 1e-06)
        w_out[...] = jnp.maximum(weights - size * projected, 0.0)
        u_w[...] = jnp.maximum(u_w[...] - size * u_p[...], 0.0)
        forward(u_w)
        r_all[me_f] = reduce_fas() - sig_own[...]
        return carry

    lax.fori_loop(0, ITERS, sweep, 0)

    turn[0:HALF, :] = r_all[me_f]
    turn[HALF:, :] = jnp.zeros((128 - HALF, 128), f32)
    turn[...] = jnp.transpose(turn[...])
    for f in range(NF):
        for r in range(2):
            fin_out[f, r * 4 : r * 4 + 4, :] = turn[r * 64 + f * 4 : r * 64 + f * 4 + 4, :]
    start_fin()
    wait_fin()
    fin_in[me_f] = fin_out[me_f]
    res_out[...] = fin_in[...]


def local(
    signal,
    initial_weights,
    coefficients,
    block_rows,
    block_cols,
    block_atoms,
    block_count,
    dictionary,
):
    i32 = jnp.int32
    rows = block_rows - lax.axis_index("vox") * ROWS
    cols = block_cols - lax.axis_index("fas") * COLS
    slots = jnp.arange(SLOTS, dtype=i32)
    lives = slots < block_count[0]
    hot = (rows[:, None] == jnp.arange(ROWS, dtype=i32)[None, :]) & lives[:, None]
    before = (slots[None, :] < slots[:, None]) & lives[None, :] & (rows[None, :] == rows[:, None])
    rank = jnp.sum(before.astype(i32), axis=1)
    count = jnp.sum(hot.astype(i32), axis=0)
    groups = (count + QUAD - 1) // QUAD
    span = jnp.arange(ROWS, dtype=i32)
    ends = jnp.sum(jnp.where(span[None, :] <= span[:, None], groups[None, :], 0), axis=1)
    firsts = ends - groups
    place = jnp.where(
        lives, jnp.sum(jnp.where(hot, firsts[None, :], 0), axis=1) * QUAD + rank, -1
    )
    turns = jnp.arange(GPAD, dtype=i32)
    grow = jnp.minimum(jnp.sum((ends[None, :] <= turns[:, None]).astype(i32), axis=1), ROWS - 1)
    is_first = jnp.any((firsts[None, :] == turns[:, None]) & (groups[None, :] > 0), axis=1)
    keep = 1.0 - is_first.astype(f32)
    last = jnp.maximum(ends - 1, 0)
    has = (groups > 0).astype(f32)
    upper = (block_atoms >= 256).astype(i32)
    digits = jnp.concatenate([block_atoms - 256 * upper, upper], axis=1).astype(bf16)
    dict_t = jnp.pad(dictionary.T, ((0, 0), (0, ATOMPAD - ATOMS)))
    w_in = initial_weights.reshape(2, 256, BF)
    w_in = jnp.concatenate([w_in[0], w_in[1]], axis=1)
    sig_in = jnp.pad(signal.reshape(8, 8, DIRS), ((0, 0), (0, 0), (0, 128 - DIRS)))

    smem = pl.BlockSpec(memory_space=pltpu.SMEM)
    vmem = pl.BlockSpec(memory_space=pltpu.VMEM)
    dma = pltpu.SemaphoreType.DMA
    w_new, res = pl.pallas_call(
        kernel,
        out_shape=(
            jax.ShapeDtypeStruct((256, 128), f32),
            jax.ShapeDtypeStruct((NF, 8, 128), f32),
        ),
        in_specs=[smem] * 4 + [pl.BlockSpec(memory_space=pl.ANY)] + [vmem] * 7,
        out_specs=(vmem, vmem),
        scratch_shapes=[
            pltpu.VMEM((SLOTS, BV * BF), bf16),
            pltpu.VMEM((2, BV * GPAD, 128), f32),
            pltpu.VMEM((SPAD, SLOTS), bf16),
            pltpu.VMEM((GPAD, 256), f32),
            pltpu.VMEM((GROUPS, BV, 256), bf16),
            pltpu.VMEM((GROUPS, DIRS, 256), bf16),
            pltpu.VMEM((COLS, SPAD), bf16),
            pltpu.VMEM((SPAD, COLS), bf16),
            pltpu.VMEM((GPAD, 256), f32),
            pltpu.VMEM((GPAD, 256), f32),
            pltpu.VMEM((GROUPS, DIRS, 128), f32),
            pltpu.VMEM((NF, HALF, 128), f32),
            pltpu.VMEM((NF, HALF, 128), f32),
            pltpu.VMEM((NF, HALF, 128), f32),
            pltpu.VMEM((ROWS, DIRS, 128), bf16),
            pltpu.VMEM((GPAD, 256), f32),
            pltpu.VMEM((SPAD, 128), bf16),
            pltpu.VMEM((2, 128, 128), f32),
            pltpu.VMEM((128, 128), f32),
            pltpu.VMEM((SIDE, 128, 128), f32),
            pltpu.VMEM((2, 128, 128), f32),
            pltpu.VMEM((COLS, 128), bf16),
            pltpu.VMEM((CHIPS, 8, 128), f32),
            pltpu.VMEM((2, 8, 128), f32),
            pltpu.VMEM((NF, 8, 128), f32),
            pltpu.VMEM((128, 128), f32),
            pltpu.VMEM((HALF, 128), f32),
            pltpu.VMEM((NF, 8, 128), f32),
            pltpu.VMEM((NF, 8, 128), f32),
        ]
        + [dma((n,)) for n in (NF, NF, NF, SIDE, CHIPS, NF, 3) for _ in range(2)]
        + [dma(())],
        compiler_params=pltpu.CompilerParams(
            collective_id=0, has_side_effects=True, vmem_limit_bytes=52 * 1024 * 1024
        ),
    )(
        grow,
        last,
        keep,
        has,
        coefficients,
        digits,
        dict_t,
        place[None, :],
        cols[None, :],
        cols[:, None],
        w_in,
        sig_in,
    )
    weights = jnp.concatenate([w_new[:, :BF], w_new[:, BF:]], axis=0).reshape(-1)
    res = res[:, :, :HALF].reshape(8, 2, 8, HALF).transpose(0, 2, 1, 3)
    return (weights, res.reshape(ROWS, 4 * DIRS))


def solution(mesh):
    placed = (
        P("vox", "fas"),
        P("fas"),
        P(("vox", "fas"), None),
        P(("vox", "fas")),
        P(("vox", "fas")),
        P(("vox", "fas"), None),
        P(("vox", "fas")),
        P(),
    )
    return jax.shard_map(
        local, mesh=mesh, in_specs=placed, out_specs=(P("fas"), P("vox", "fas")), check_vma=False
    )
```

time: 333 us -> 264 us (0.79)
  Pallas kernels: 306 us -> 255 us
  local copies, waits for them, and re-layouts: 15.7 us -> 4.72 us
  other arithmetic: 9.65 us -> 2.38 us
    pallas_call x1, Pallas kernels: 306 us -> 255 us  [local(): pl.pallas_call(kernel, out_shape=(jax.ShapeDtypeStruct((256, 128), f32),...]
    concatenate x1, other arithmetic: 7.04 us -> 0.09 us  [local(): jnp.concatenate([block_atoms - 256 * upper, upper], axis=1).astype(bf16)]
    reshape x3 -> x0, local copies, waits for them, and re-layouts: 6.88 us -> none  [the longest x1 6.69 us: local(): coef = coefficients.reshape(SLOTS, BV, BF)]
    unnamed x12 -> x3, local copies, waits for them, and re-layouts: 5.56 us -> 0.94 us
where the time goes in v2:
time: 264 us; the launch traced here: 263 us
  Pallas kernels  255 us (97%)
  local copies, waits for them, and re-layouts  4.72 us (2%)
    pallas_call x1, Pallas kernels, local(): pl.pallas_call(kernel, out_shape=(jax.ShapeDtypeStruct((256, 128), f32),...  255 us

profile of v2, /device:TPU:0, one launch (start us, length us, event | category | flops | bytes accessed | tf_op | source)
XLA Modules:
  0.0 263.4 jit_solution(860442610863474131)
XLA Ops:
  0.6 0.0 copy-start
  0.6 0.7 broadcast_subtract_fusion.1
  2.0 0.1 convert_reduce_fusion.1
  2.1 0.1 select_reduce_fusion.1
  2.3 0.1 select_reduce_fusion
  2.3 0.2 convert_reduce_fusion
  2.6 0.1 fusion.4
  2.7 0.1 convert_reduce_fusion.2
  2.8 0.9 fusion.7
  3.6 0.1 slice.38
  3.7 0.1 slice.40
  3.8 0.1 pad_maximum_fusion.1.w_in
  3.9 0.9 copy.18
  4.9 0.1 pad_maximum_fusion.2.digits
  5.0 0.7 broadcast_subtract_fusion
  5.7 0.1 copy.19.cols_sub
  5.9 0.9 pad.8.dict_t
  6.8 0.0 copy-done
  6.8 0.1 reshape.100
  6.9 254.9 %shard_map.95 = (f32[256,128]{1,0:T(8,128)S(1)}, f32[16,8,128]{2,1,0:T(8,128)S(1)}) custom-call(s32[80]{0:T(128)S(1)} %broadcast_minimum_fusion.grow, s32[16]{0:T(128)S(1)} %get-tuple-element.13.last, f32[80]{0:T(128)S(1)} %convert_subtract_fusion.keep, f32[16]{0:T(128)S(1)} %get-tuple-element.6.has, bf16[256,4096]{1,0:T(8,128)(2,1)} %coef_hbm.1, ...), custom_call_target="tpu_custom_call" | custom-call | tf_op jit(solution)/shard_map/pallas_call | solution.py:444
  261.7 0.1 fusion.6
  261.9 0.8 reshape.101
  262.7 0.7 reshape.103
  (13 shorter events, 0.2 us)
Async XLA Ops:
  0.6 6.1 %copy-start = (f32[16,384]{1,0:T(8,128)S(1)}, f32[16,384]{1,0:T(8,128)}, u32[]{:S(2)}) copy-start(f32[16,384]{1,0:T(8,128)} %param.8) | copy-start | bytes 73732

commit v3 on v2

--- a/solution.py
+++ b/solution.py
@@ -23,6 +23,7 @@
 SPAD = 384
 ATOMPAD = 384
 HALF = DIRS // 2
+PIECE = HALF // 2
 
 
 def hops(off):
@@ -81,6 +82,7 @@
     sel_t,
     u_p,
     u_w,
+    table,
     buf,
     part,
     rs_in,
@@ -160,6 +162,12 @@
             )
         return pair(out, arrive)
 
+    def half_copies(src_at, dst, send_sem, recv_sem):
+        return [
+            copies(lambda p: src_at(h, p), dst.at[h], send_sem.at[h], recv_sem.at[h])
+            for h in range(2)
+        ]
+
     def other_fas(off):
         return lax.rem(me_f // SIDE + off[0], SIDE) * SIDE + lax.rem(me_f + off[1], SIDE)
 
@@ -194,7 +202,9 @@
     def name_atoms(g, carry):
         row = names[pl.ds(g, 1), :].astype(jnp.int32)
         hot = (lax.broadcasted_iota(jnp.int32, (ATOMPAD, 256), 0) == row).astype(f32).astype(bf16)
-        at[g] = jnp.dot(dict_t[...], hot, preferred_element_type=f32).astype(bf16)
+        made = jnp.dot(dict_t[...], hot, preferred_element_type=f32).astype(bf16)
+        at[0, g] = made[:HALF]
+        at[1, g] = made[HALF:]
         return carry
 
     lax.fori_loop(0, GROUPS, name_atoms, 0, unroll=4)
@@ -250,41 +260,73 @@
         u_ref[:, 0:128] = jnp.where(mask, got[0:GPAD], got[GPAD : 2 * GPAD])
         u_ref[:, 128:256] = jnp.where(mask, got[2 * GPAD : 3 * GPAD], got[3 * GPAD : 4 * GPAD])
 
-    def forward(u_ref):
-        def step(g, acc):
-            scaled = cg[g].astype(f32) * u_ref[pl.ds(g, 1), :]
-            high = scaled.astype(bf16)
-            low = (scaled - high.astype(f32)).astype(bf16)
-            both = jnp.concatenate([high, low], axis=0)
+    def forward(u_ref, exact):
+        lanes = 128 if exact else 64
+
+        def finish(g, acc, h, block):
             made = lax.dot_general(
-                at[g], both, (((1,), (1,)), ((), ())), preferred_element_type=f32
+                at[h, g], block, (((1,), (1,)), ((), ())), preferred_element_type=f32
             )
             acc = acc * keep[g] + made
-            buf[g] = acc
+            buf[h, g, :, 0:lanes] = acc
             return acc
 
-        lax.fori_loop(0, GROUPS, step, jnp.zeros((DIRS, 128), f32), unroll=19)
-        mask = low_lanes((DIRS, 128))
-        for pair in range(ROWS // 2):
-            even = fold(buf[last[2 * pair]] * has[2 * pair])
-            odd = fold(buf[last[2 * pair + 1]] * has[2 * pair + 1])
-            both = jnp.where(mask, even, odd)
-            part[2 * pair] = both[:HALF]
-            part[2 * pair + 1] = both[HALF:]
-
-    start_rs, wait_rs = copies(lambda p: part.at[p], rs_in, s_rs, r_rs)
-    start_ag, wait_ag = copies(lambda p: r_all.at[me_f], r_all, s_ag, r_ag)
+        def first(g, acc):
+            scaled = cg[g].astype(f32) * u_ref[pl.ds(g, 1), :]
+            block = scaled.astype(bf16)
+            if exact:
+                low = (scaled - block.astype(f32)).astype(bf16)
+                block = jnp.concatenate([block, low], axis=0)
+            table[g, 0:lanes, :] = block
+            return finish(g, acc, 0, block)
+
+        def second(g, acc):
+            return finish(g, acc, 1, table[g, 0:lanes, :])
+
+        mask = low_lanes((HALF, 128))
+        for h, step in ((0, first), (1, second)):
+            lax.fori_loop(0, GROUPS, step, jnp.zeros((HALF, lanes), f32), unroll=19)
+            for two in range(ROWS // 2):
+                even = buf[h, last[2 * two]] * has[2 * two]
+                odd = buf[h, last[2 * two + 1]] * has[2 * two + 1]
+                if exact:
+                    both = jnp.where(mask, fold(even), fold(odd))
+                else:
+                    both = jnp.where(mask, even, pltpu.roll(odd, 64, 1))
+                part[h, 2 * two] = both[:PIECE]
+                part[h, 2 * two + 1] = both[PIECE:]
+            rs[h][0]()
+
+    def summed(h):
+        rs[h][1]()
+        total = part[h, me_f]
+        for off in range(1, NF):
+            total = total + rs_in[h, lax.rem(me_f + off, NF)]
+        return total
+
+    def gather_residual(start):
+        for h in range(2):
+            r_all[h, me_f] = summed(h) - sig_own[h]
+            pl.when(start)(ag[h][0])
+
+    rs = half_copies(lambda h, p: part.at[h, p], rs_in, s_rs, r_rs)
+    ag = half_copies(lambda h, p: r_all.at[h, me_f], r_all, s_ag, r_ag)
     start_fin, wait_fin = copies(lambda p: fin_out.at[p], fin_in, s_fin, r_fin)
 
-    start_swap, wait_swap = with_twin(g_part.at[1 - me_c], g_pair, g_pair, 0)
-    start_back, wait_back = with_twin(g_all.at[me_c], g_all.at[me_c], g_all.at[1 - me_c], 1)
-    out, arrive = [], []
-    for off in (2, 1, 3):
-        y = lax.rem(me_y + off, SIDE)
-        where = {"vox": y * 2 + me_c}
-        out.append(remote(g_in.at[me_y], g_in.at[me_y], s_gr.at[y], r_gr.at[me_y], where))
-        arrive.append(remote(g_in.at[y], g_in.at[y], s_gr.at[y], r_gr.at[y], where))
-    start_gr, wait_gr = pair(out, arrive)
+    swap, along_y, back = [], [], []
+    for h in range(2):
+        landing = g_pair.at[h]
+        swap.append(with_twin(g_part.at[1 - me_c, h], landing, landing, h))
+        own, other = g_all.at[me_c, h], g_all.at[1 - me_c, h]
+        back.append(with_twin(own, own, other, 2 + h))
+        out, arrive = [], []
+        for off in (2, 1, 3):
+            y = lax.rem(me_y + off, SIDE)
+            where = {"vox": y * 2 + me_c}
+            own, other = g_in.at[h, me_y], g_in.at[h, y]
+            out.append(remote(own, own, s_gr.at[h, y], r_gr.at[h, me_y], where))
+            arrive.append(remote(own, other, s_gr.at[h, y], r_gr.at[h, y], where))
+        along_y.append(pair(out, arrive))
 
     mine = me_y * NF + me_f
     out, arrive = [], []
@@ -297,76 +339,74 @@
         src = sc_in.at[chip, 0:1]
         arrive.append(remote(src, src, s_sc.at[chip], r_sc.at[chip], where))
     start_sc, wait_sc = pair(out, arrive)
-    start_two, wait_two = with_twin(sc_pair.at[me_c], sc_pair.at[me_c], sc_pair.at[1 - me_c], 2)
-
-    def added():
-        total = part[me_f]
-        for off in range(1, NF):
-            total = total + rs_in[lax.rem(me_f + off, NF)]
-        return total
-
-    def reduce_fas():
-        start_rs()
-        wait_rs()
-        return added()
+    start_two, wait_two = with_twin(sc_pair.at[me_c], sc_pair.at[me_c], sc_pair.at[1 - me_c], 4)
 
     w_out[...] = w_in[...]
     gather(w_in[...], u_w)
-    forward(u_w)
-    start_rs()
+    forward(u_w, True)
     wait_sig()
     sg_in[me_f] = sig_in[me_f // 2]
     for f in range(NF):
         for r in range(2):
             turn[r * 64 + f * 4 : r * 64 + f * 4 + 4, :] = sg_in[f, r * 4 : r * 4 + 4, :]
     turn[...] = jnp.transpose(turn[...])
-    half_at = pl.multiple_of(lax.rem(me_f, 2) * HALF, 8)
-    sig_own[...] = turn[pl.ds(half_at, HALF), :]
-    wait_rs()
-    r_all[me_f] = added() - sig_own[...]
-
-    def sweep(_, carry):
-        start_ag()
-        wait_ag()
-        for pair in range(ROWS // 2):
-            x = jnp.concatenate([r_all[2 * pair], r_all[2 * pair + 1]], axis=0)
+    for h in range(2):
+        first_row = pl.multiple_of(h * HALF + lax.rem(me_f, 2) * PIECE, 8)
+        sig_own[h] = turn[pl.ds(first_row, PIECE), :]
+    gather_residual(me_f >= 0)
+
+    def backward(h):
+        for two in range(ROWS // 2):
+            x = jnp.concatenate([r_all[h, 2 * two], r_all[h, 2 * two + 1]], axis=0)
             even, odd = split_pair(x)
-            r_two[2 * pair] = even
-            r_two[2 * pair + 1] = odd
+            r_two[h, 2 * two] = even
+            r_two[h, 2 * two + 1] = odd
 
         def step(g, c):
             block = cg[g]
             twice = jnp.concatenate([block, block], axis=0)
-            inner = jnp.dot(r_two[grow[g]], twice, preferred_element_type=f32)
-            contrib[pl.ds(g, 1), :] = jnp.sum(inner * at[g].astype(f32), axis=0, keepdims=True)
+            inner = jnp.dot(r_two[h, grow[g]], twice, preferred_element_type=f32)
+            row = jnp.sum(inner * at[h, g].astype(f32), axis=0, keepdims=True)
+            contrib[pl.ds(g, 1), :] = row if h == 0 else contrib[pl.ds(g, 1), :] + row
             return c
 
         lax.fori_loop(0, GROUPS, step, 0, unroll=19)
+
+    def sweep(turns, carry):
+        for h in range(2):
+            ag[h][1]()
+            backward(h)
         for half in range(2):
             first, second = split_pair(contrib[:, half * 128 : (half + 1) * 128])
             b_two[2 * half * GPAD : (2 * half + 1) * GPAD, :] = first
             b_two[(2 * half + 1) * GPAD : (2 * half + 2) * GPAD, :] = second
         got = fold(jnp.dot(sel[...], b_two[...], preferred_element_type=f32))
         mask = low_lanes((256, 128))
-        g_part[...] = jnp.where(mask, got[0:256], got[256:512]).reshape(2, 128, 128)
-        start_swap()
-        wait_swap()
-        g_in[me_y] = g_part[me_c] + g_pair[...]
-        start_gr()
-        wait_gr()
-        g_all[me_c] = (g_in[0] + g_in[1]) + (g_in[2] + g_in[3])
-        start_back()
-        wait_back()
+        g_part[...] = jnp.where(mask, got[0:256], got[256:512]).reshape(2, 2, 64, 128)
+        for h in range(2):
+            swap[h][0]()
+        for h in range(2):
+            swap[h][1]()
+            g_in[h, me_y] = g_part[me_c, h] + g_pair[h]
+            along_y[h][0]()
+        for h in range(2):
+            along_y[h][1]()
+            g_all[me_c, h] = (g_in[h, 0] + g_in[h, 1]) + (g_in[h, 2] + g_in[h, 3])
+            back[h][0]()
+        for h in range(2):
+            back[h][1]()
         weights = w_out[...]
         gradient = g_all[...].reshape(256, 128)
         projected = jnp.where((weights > 0) | (gradient < 0), gradient, 0.0)
         gather(projected, u_p)
-        forward(u_p)
-        image = reduce_fas()
-        squares = jnp.sum((image * image).reshape(6, 8, 128), axis=0)
+        forward(u_p, False)
         steep = jnp.sum((projected * projected).reshape(32, 8, 128), axis=0)
+        steep = jnp.sum(fold(steep), axis=0, keepdims=True)
+        squares = jnp.zeros((8, 128), f32)
+        for h in range(2):
+            image = summed(h)
+            squares = squares + jnp.sum((image * image).reshape(PIECE // 8, 8, 128), axis=0)
         squares = jnp.sum(fold(squares), axis=0, keepdims=True)
-        steep = jnp.sum(fold(steep), axis=0, keepdims=True)
         sc_in[mine, 0:1, :] = jnp.where(low_lanes((1, 128)), squares, steep)
         start_sc()
         wait_sc()
@@ -381,13 +421,14 @@
         size = grad_sq / (image_sq + 1e-06)
         w_out[...] = jnp.maximum(weights - size * projected, 0.0)
         u_w[...] = jnp.maximum(u_w[...] - size * u_p[...], 0.0)
-        forward(u_w)
-        r_all[me_f] = reduce_fas() - sig_own[...]
+        forward(u_w, True)
+        gather_residual(turns < ITERS - 1)
         return carry
 
     lax.fori_loop(0, ITERS, sweep, 0)
 
-    turn[0:HALF, :] = r_all[me_f]
+    turn[0:PIECE, :] = r_all[0, me_f]
+    turn[PIECE:HALF, :] = r_all[1, me_f]
     turn[HALF:, :] = jnp.zeros((128 - HALF, 128), f32)
     turn[...] = jnp.transpose(turn[...])
     for f in range(NF):
@@ -455,32 +496,37 @@
             pltpu.VMEM((SPAD, SLOTS), bf16),
             pltpu.VMEM((GPAD, 256), f32),
             pltpu.VMEM((GROUPS, BV, 256), bf16),
-            pltpu.VMEM((GROUPS, DIRS, 256), bf16),
+            pltpu.VMEM((2, GROUPS, HALF, 256), bf16),
             pltpu.VMEM((COLS, SPAD), bf16),
             pltpu.VMEM((SPAD, COLS), bf16),
             pltpu.VMEM((GPAD, 256), f32),
             pltpu.VMEM((GPAD, 256), f32),
-            pltpu.VMEM((GROUPS, DIRS, 128), f32),
-            pltpu.VMEM((NF, HALF, 128), f32),
-            pltpu.VMEM((NF, HALF, 128), f32),
-            pltpu.VMEM((NF, HALF, 128), f32),
-            pltpu.VMEM((ROWS, DIRS, 128), bf16),
+            pltpu.VMEM((GROUPS, 128, 256), bf16),
+            pltpu.VMEM((2, GROUPS, HALF, 128), f32),
+            pltpu.VMEM((2, NF, PIECE, 128), f32),
+            pltpu.VMEM((2, NF, PIECE, 128), f32),
+            pltpu.VMEM((2, NF, PIECE, 128), f32),
+            pltpu.VMEM((2, ROWS, HALF, 128), bf16),
             pltpu.VMEM((GPAD, 256), f32),
             pltpu.VMEM((SPAD, 128), bf16),
-            pltpu.VMEM((2, 128, 128), f32),
-            pltpu.VMEM((128, 128), f32),
-            pltpu.VMEM((SIDE, 128, 128), f32),
-            pltpu.VMEM((2, 128, 128), f32),
+            pltpu.VMEM((2, 2, 64, 128), f32),
+            pltpu.VMEM((2, 64, 128), f32),
+            pltpu.VMEM((2, SIDE, 64, 128), f32),
+            pltpu.VMEM((2, 2, 64, 128), f32),
             pltpu.VMEM((COLS, 128), bf16),
             pltpu.VMEM((CHIPS, 8, 128), f32),
             pltpu.VMEM((2, 8, 128), f32),
             pltpu.VMEM((NF, 8, 128), f32),
             pltpu.VMEM((128, 128), f32),
-            pltpu.VMEM((HALF, 128), f32),
+            pltpu.VMEM((2, PIECE, 128), f32),
             pltpu.VMEM((NF, 8, 128), f32),
             pltpu.VMEM((NF, 8, 128), f32),
         ]
-        + [dma((n,)) for n in (NF, NF, NF, SIDE, CHIPS, NF, 3) for _ in range(2)]
+        + [
+            dma(n)
+            for n in ((NF,), (2, NF), (2, NF), (2, SIDE), (CHIPS,), (NF,), (5,))
+            for _ in range(2)
+        ]
         + [dma(())],
         compiler_params=pltpu.CompilerParams(
             collective_id=0, has_side_effects=True, vmem_limit_bytes=52 * 1024 * 1024
@@ -500,7 +546,7 @@
         sig_in,
     )
     weights = jnp.concatenate([w_new[:, :BF], w_new[:, BF:]], axis=0).reshape(-1)
-    res = res[:, :, :HALF].reshape(8, 2, 8, HALF).transpose(0, 2, 1, 3)
+    res = res[:, :, :HALF].reshape(8, 2, 8, 2, PIECE).transpose(0, 2, 3, 1, 4)
     return (weights, res.reshape(ROWS, 4 * DIRS))
 
 

time: 264 us -> 256 us (0.970)
  Pallas kernels: 255 us -> 247 us
    pallas_call x1, Pallas kernels: 255 us -> 247 us  [local(): pl.pallas_call(kernel, out_shape=(jax.ShapeDtypeStruct((256, 128), f32),...]
where the time goes in v3:
time: 256 us; the launch traced here: 255 us
  Pallas kernels  247 us (96%)
  local copies, waits for them, and re-layouts  4.95 us (2%)
    pallas_call x1, Pallas kernels, local(): pl.pallas_call(kernel, out_shape=(jax.ShapeDtypeStruct((256, 128), f32),...  247 us

profile of v3, /device:TPU:0, one launch (start us, length us, event | category | flops | bytes accessed | tf_op | source)
XLA Modules:
  0.0 255.3 jit_solution(3550644801084769523)
XLA Ops:
  0.6 0.0 copy-start
  0.6 0.7 broadcast_subtract_fusion.1
  2.0 0.1 convert_reduce_fusion.1
  2.1 0.1 select_reduce_fusion.1
  2.3 0.1 select_reduce_fusion
  2.3 0.2 convert_reduce_fusion
  2.6 0.1 fusion.4
  2.7 0.1 convert_reduce_fusion.2
  2.8 0.9 fusion.7
  3.6 0.1 slice.38
  3.7 0.1 slice.40
  3.8 0.1 pad_maximum_fusion.1.w_in
  3.9 0.9 copy.18
  4.9 0.1 pad_maximum_fusion.2.digits
  5.0 0.7 broadcast_subtract_fusion
  5.7 0.1 copy.19.cols_sub
  5.9 0.9 pad.8.dict_t
  6.8 0.0 copy-done
  6.8 0.1 reshape.100
  6.9 246.5 %shard_map.95 = (f32[256,128]{1,0:T(8,128)S(1)}, f32[16,8,128]{2,1,0:T(8,128)S(1)}) custom-call(s32[80]{0:T(128)S(1)} %broadcast_minimum_fusion.grow, s32[16]{0:T(128)S(1)} %get-tuple-element.13.last, f32[80]{0:T(128)S(1)} %convert_subtract_fusion.keep, f32[16]{0:T(128)S(1)} %get-tuple-element.6.has, bf16[256,4096]{1,0:T(8,128)(2,1)} %coef_hbm.1, ...), custom_call_target="tpu_custom_call" | custom-call | tf_op jit(solution)/shard_map/pallas_call | solution.py:485
  253.4 0.1 fusion.6
  253.5 0.8 reshape.101
  254.3 0.1 reshape.102
  254.4 0.1 copy.20
  254.5 0.8 reshape.103
  (12 shorter events, 0.1 us)
Async XLA Ops:
  0.6 6.1 %copy-start = (f32[16,384]{1,0:T(8,128)S(1)}, f32[16,384]{1,0:T(8,128)}, u32[]{:S(2)}) copy-start(f32[16,384]{1,0:T(8,128)} %param.8) | copy-start | bytes 73732

commit v4 on v3

--- a/solution.py
+++ b/solution.py
@@ -285,7 +285,7 @@
 
         mask = low_lanes((HALF, 128))
         for h, step in ((0, first), (1, second)):
-            lax.fori_loop(0, GROUPS, step, jnp.zeros((HALF, lanes), f32), unroll=19)
+            lax.fori_loop(0, GROUPS, step, jnp.zeros((HALF, lanes), f32), unroll=76)
             for two in range(ROWS // 2):
                 even = buf[h, last[2 * two]] * has[2 * two]
                 odd = buf[h, last[2 * two + 1]] * has[2 * two + 1]
@@ -370,7 +370,7 @@
             contrib[pl.ds(g, 1), :] = row if h == 0 else contrib[pl.ds(g, 1), :] + row
             return c
 
-        lax.fori_loop(0, GROUPS, step, 0, unroll=19)
+        lax.fori_loop(0, GROUPS, step, 0, unroll=76)
 
     def sweep(turns, carry):
         for h in range(2):

time: 256 us -> 247 us (0.965)
  Pallas kernels: 247 us -> 238 us
    pallas_call x1, Pallas kernels: 247 us -> 238 us  [local(): pl.pallas_call(kernel, out_shape=(jax.ShapeDtypeStruct((256, 128), f32),...]
where the time goes in v4:
time: 247 us
  Pallas kernels  238 us (96%)
  local copies, waits for them, and re-layouts  4.95 us (2%)
    pallas_call x1, Pallas kernels, local(): pl.pallas_call(kernel, out_shape=(jax.ShapeDtypeStruct((256, 128), f32),...  238 us

profile of v4, /device:TPU:0, one launch (start us, length us, event | category | flops | bytes accessed | tf_op | source)
XLA Modules:
  0.0 246.9 jit_solution(411068149202443022)
XLA Ops:
  0.6 0.0 copy-start
  0.6 0.7 broadcast_subtract_fusion.1
  2.0 0.1 convert_reduce_fusion.1
  2.1 0.1 select_reduce_fusion.1
  2.3 0.1 select_reduce_fusion
  2.3 0.2 convert_reduce_fusion
  2.6 0.1 fusion.4
  2.7 0.1 convert_reduce_fusion.2
  2.8 0.9 fusion.7
  3.6 0.1 slice.38
  3.7 0.1 slice.40
  3.8 0.1 pad_maximum_fusion.1.w_in
  3.9 0.9 copy.18
  4.9 0.1 pad_maximum_fusion.2.digits
  5.0 0.7 broadcast_subtract_fusion
  5.7 0.1 copy.19.cols_sub
  5.9 0.9 pad.8.dict_t
  6.8 0.0 copy-done
  6.8 0.1 reshape.100
  6.9 238.1 %shard_map.95 = (f32[256,128]{1,0:T(8,128)S(1)}, f32[16,8,128]{2,1,0:T(8,128)S(1)}) custom-call(s32[80]{0:T(128)S(1)} %broadcast_minimum_fusion.grow, s32[16]{0:T(128)S(1)} %get-tuple-element.13.last, f32[80]{0:T(128)S(1)} %convert_subtract_fusion.keep, f32[16]{0:T(128)S(1)} %get-tuple-element.6.has, bf16[256,4096]{1,0:T(8,128)(2,1)} %coef_hbm.1, ...), custom_call_target="tpu_custom_call" | custom-call | tf_op jit(solution)/shard_map/pallas_call | solution.py:485
  245.0 0.1 fusion.6
  245.1 0.8 reshape.101
  245.9 0.1 reshape.102
  246.0 0.1 copy.20
  246.1 0.8 reshape.103
  (12 shorter events, 0.1 us)
Async XLA Ops:
  0.6 6.1 %copy-start = (f32[16,384]{1,0:T(8,128)S(1)}, f32[16,384]{1,0:T(8,128)}, u32[]{:S(2)}) copy-start(f32[16,384]{1,0:T(8,128)} %param.8) | copy-start | bytes 73732

commit v5 on v4

--- a/solution.py
+++ b/solution.py
@@ -142,12 +142,14 @@
                 c.start()
 
         def wait():
-            for c in arrive:
+            for c in reversed(arrive):
                 c.wait_recv()
-            for c in out:
+
+        def sent():
+            for c in reversed(out):
                 c.wait_send()
 
-        return start, wait
+        return start, wait, sent
 
     def copies(src_at, dst, send_sem, recv_sem):
         out, arrive = [], []
@@ -207,7 +209,7 @@
         at[1, g] = made[HALF:]
         return carry
 
-    lax.fori_loop(0, GROUPS, name_atoms, 0, unroll=4)
+    lax.fori_loop(0, GROUPS, name_atoms, 0, unroll=19)
     where_col = (lax.broadcasted_iota(jnp.int32, (COLS, SLOTS), 0) == cols_lane[...]).astype(f32)
     sel[...] = lax.dot_general(
         where_col.astype(bf16), pick[...], (((1,), (1,)), ((), ())), preferred_element_type=f32
@@ -220,7 +222,7 @@
     b_two[...] = jnp.zeros_like(b_two)
 
     pl.semaphore_wait(barrier, CHIPS)
-    start_sig, wait_sig = copies(lambda p: sig_in.at[p // 2], sg_in, s_sig, r_sig)
+    start_sig, wait_sig, sent_sig = copies(lambda p: sig_in.at[p // 2], sg_in, s_sig, r_sig)
     start_sig()
 
     fetch.wait()
@@ -240,7 +242,7 @@
             wide[half, pl.ds(first + GPAD, GPAD), :] = odd
         return carry
 
-    lax.fori_loop(0, BV // 2, spread, 0, unroll=4)
+    lax.fori_loop(0, BV // 2, spread, 0, unroll=8)
 
     def bring(g, carry):
         for half in range(2):
@@ -248,7 +250,7 @@
             cg[g, :, half * 128 : half * 128 + 128] = block.astype(bf16)
         return carry
 
-    lax.fori_loop(0, GROUPS, bring, 0, unroll=4)
+    lax.fori_loop(0, GROUPS, bring, 0, unroll=19)
 
 
     def gather(values, u_ref):
@@ -311,7 +313,7 @@
 
     rs = half_copies(lambda h, p: part.at[h, p], rs_in, s_rs, r_rs)
     ag = half_copies(lambda h, p: r_all.at[h, me_f], r_all, s_ag, r_ag)
-    start_fin, wait_fin = copies(lambda p: fin_out.at[p], fin_in, s_fin, r_fin)
+    start_fin, wait_fin, sent_fin = copies(lambda p: fin_out.at[p], fin_in, s_fin, r_fin)
 
     swap, along_y, back = [], [], []
     for h in range(2):
@@ -338,8 +340,8 @@
         out.append(remote(src, src, s_sc.at[chip], r_sc.at[mine], where))
         src = sc_in.at[chip, 0:1]
         arrive.append(remote(src, src, s_sc.at[chip], r_sc.at[chip], where))
-    start_sc, wait_sc = pair(out, arrive)
-    start_two, wait_two = with_twin(sc_pair.at[me_c], sc_pair.at[me_c], sc_pair.at[1 - me_c], 4)
+    start_sc, wait_sc, sent_sc = pair(out, arrive)
+    start_two, wait_two, sent_two = with_twin(sc_pair.at[me_c], sc_pair.at[me_c], sc_pair.at[1 - me_c], 4)
 
     w_out[...] = w_in[...]
     gather(w_in[...], u_w)
@@ -374,17 +376,30 @@
 
     def sweep(turns, carry):
         for h in range(2):
+            rs[h][2]()
+        for h in range(2):
             ag[h][1]()
             backward(h)
         for half in range(2):
             first, second = split_pair(contrib[:, half * 128 : (half + 1) * 128])
             b_two[2 * half * GPAD : (2 * half + 1) * GPAD, :] = first
             b_two[(2 * half + 1) * GPAD : (2 * half + 2) * GPAD, :] = second
-        got = fold(jnp.dot(sel[...], b_two[...], preferred_element_type=f32))
-        mask = low_lanes((256, 128))
-        g_part[...] = jnp.where(mask, got[0:256], got[256:512]).reshape(2, 2, 64, 128)
-        for h in range(2):
+
+        def produce(core, h):
+            at_row = pl.multiple_of(core * 128 + h * 64, 64)
+            near = sel[pl.ds(at_row, 64), :]
+            far = sel[pl.ds(at_row + 256, 64), :]
+            got = jnp.concatenate([near, far], axis=0)
+            got = fold(jnp.dot(got, b_two[...], preferred_element_type=f32))
+            g_part[core, h] = jnp.where(low_lanes((64, 128)), got[0:64], got[64:128])
+
+        for h in range(2):
+            produce(1 - me_c, h)
             swap[h][0]()
+        for h in range(2):
+            produce(me_c, h)
+        for h in range(2):
+            ag[h][2]()
         for h in range(2):
             swap[h][1]()
             g_in[h, me_y] = g_part[me_c, h] + g_pair[h]
@@ -400,6 +415,9 @@
         projected = jnp.where((weights > 0) | (gradient < 0), gradient, 0.0)
         gather(projected, u_p)
         forward(u_p, False)
+        for stage in (swap, along_y, back):
+            for h in range(2):
+                stage[h][2]()
         steep = jnp.sum((projected * projected).reshape(32, 8, 128), axis=0)
         steep = jnp.sum(fold(steep), axis=0, keepdims=True)
         squares = jnp.zeros((8, 128), f32)
@@ -409,6 +427,8 @@
         squares = jnp.sum(fold(squares), axis=0, keepdims=True)
         sc_in[mine, 0:1, :] = jnp.where(low_lanes((1, 128)), squares, steep)
         start_sc()
+        for h in range(2):
+            rs[h][2]()
         wait_sc()
         sums = jnp.sum(sc_in[:, 0, :], axis=0, keepdims=True)
         sc_pair[me_c] = jnp.broadcast_to(sums, (8, 128))
@@ -422,10 +442,14 @@
         w_out[...] = jnp.maximum(weights - size * projected, 0.0)
         u_w[...] = jnp.maximum(u_w[...] - size * u_p[...], 0.0)
         forward(u_w, True)
+        sent_sc()
+        sent_two()
         gather_residual(turns < ITERS - 1)
         return carry
 
     lax.fori_loop(0, ITERS, sweep, 0)
+    for h in range(2):
+        rs[h][2]()
 
     turn[0:PIECE, :] = r_all[0, me_f]
     turn[PIECE:HALF, :] = r_all[1, me_f]
@@ -436,6 +460,8 @@
             fin_out[f, r * 4 : r * 4 + 4, :] = turn[r * 64 + f * 4 : r * 64 + f * 4 + 4, :]
     start_fin()
     wait_fin()
+    sent_fin()
+    sent_sig()
     fin_in[me_f] = fin_out[me_f]
     res_out[...] = fin_in[...]
 

time: 247 us -> 239 us (0.968)
  Pallas kernels: 238 us -> 229 us
    pallas_call x1, Pallas kernels: 238 us -> 229 us  [local(): pl.pallas_call(kernel, out_shape=(jax.ShapeDtypeStruct((256, 128), f32),...]
where the time goes in v5:
time: 239 us; the launch traced here: 238 us
  Pallas kernels  229 us (96%)
  local copies, waits for them, and re-layouts  4.95 us (2%)
    pallas_call x1, Pallas kernels, local(): pl.pallas_call(kernel, out_shape=(jax.ShapeDtypeStruct((256, 128), f32),...  229 us

profile of v5, /device:TPU:0, one launch (start us, length us, event | category | flops | bytes accessed | tf_op | source)
XLA Modules:
  0.0 237.9 jit_solution(13020460997979734485)
XLA Ops:
  0.6 0.0 copy-start
  0.6 0.7 broadcast_subtract_fusion.1
  2.0 0.1 convert_reduce_fusion.1
  2.1 0.1 select_reduce_fusion.1
  2.3 0.1 select_reduce_fusion
  2.3 0.2 convert_reduce_fusion
  2.6 0.1 fusion.4
  2.7 0.1 convert_reduce_fusion.2
  2.8 0.9 fusion.7
  3.6 0.1 slice.38
  3.7 0.1 slice.40
  3.8 0.1 pad_maximum_fusion.1.w_in
  3.9 0.9 copy.18
  4.9 0.1 pad_maximum_fusion.2.digits
  5.0 0.7 broadcast_subtract_fusion
  5.7 0.1 copy.19.cols_sub
  5.9 0.9 pad.8.dict_t
  6.8 0.0 copy-done
  6.8 0.1 reshape.100
  6.9 229.1 %shard_map.95 = (f32[256,128]{1,0:T(8,128)S(1)}, f32[16,8,128]{2,1,0:T(8,128)S(1)}) custom-call(s32[80]{0:T(128)S(1)} %broadcast_minimum_fusion.grow, s32[16]{0:T(128)S(1)} %get-tuple-element.13.last, f32[80]{0:T(128)S(1)} %convert_subtract_fusion.keep, f32[16]{0:T(128)S(1)} %get-tuple-element.6.has, bf16[256,4096]{1,0:T(8,128)(2,1)} %coef_hbm.1, ...), custom_call_target="tpu_custom_call" | custom-call | tf_op jit(solution)/shard_map/pallas_call | solution.py:511
  236.0 0.1 fusion.6
  236.1 0.8 reshape.101
  236.9 0.1 reshape.102
  237.0 0.1 copy.20
  237.1 0.8 reshape.103
  (12 shorter events, 0.1 us)
Async XLA Ops:
  0.6 6.1 %copy-start = (f32[16,384]{1,0:T(8,128)S(1)}, f32[16,384]{1,0:T(8,128)}, u32[]{:S(2)}) copy-start(f32[16,384]{1,0:T(8,128)} %param.8) | copy-start | bytes 73732

commit v6 on v5

--- a/solution.py
+++ b/solution.py
@@ -64,7 +64,7 @@
     has,
     coef_hbm,
     digits,
-    dict_t,
+    words,
     place_lane,
     cols_lane,
     cols_sub,
@@ -75,6 +75,7 @@
     coef,
     wide,
     pick,
+    dict_t,
     names,
     cg,
     at,
@@ -201,6 +202,10 @@
     names[:, 0:128] = jnp.where(mask, found[0:GPAD], found[GPAD : 2 * GPAD])
     names[:, 128:256] = jnp.where(mask, found[2 * GPAD : 3 * GPAD], found[3 * GPAD :])
 
+    for k in range(ATOMPAD // 128):
+        block = jnp.transpose(words[k * 128 : (k + 1) * 128, :].astype(f32))
+        dict_t[:, k * 128 : (k + 1) * 128] = block[:DIRS].astype(bf16)
+
     def name_atoms(g, carry):
         row = names[pl.ds(g, 1), :].astype(jnp.int32)
         hot = (lax.broadcasted_iota(jnp.int32, (ATOMPAD, 256), 0) == row).astype(f32).astype(bf16)
@@ -463,7 +468,13 @@
     sent_fin()
     sent_sig()
     fin_in[me_f] = fin_out[me_f]
-    res_out[...] = fin_in[...]
+    lane = lax.broadcasted_iota(jnp.int32, (8, 128), 1)
+    for two in range(ROWS // 2):
+        a, b = fin_in[2 * two], fin_in[2 * two + 1]
+        out = jnp.where(lane < PIECE, a, pltpu.roll(b, PIECE, 1))
+        out = jnp.where(lane < 2 * PIECE, out, pltpu.roll(a, PIECE, 1))
+        out = jnp.where(lane < 3 * PIECE, out, pltpu.roll(b, 2 * PIECE, 1))
+        res_out[two] = out[:, :DIRS]
 
 
 def local(
@@ -477,8 +488,9 @@
     dictionary,
 ):
     i32 = jnp.int32
-    rows = block_rows - lax.axis_index("vox") * ROWS
-    cols = block_cols - lax.axis_index("fas") * COLS
+    rows = block_rows & (ROWS - 1)
+    cols = block_cols & (COLS - 1)
+    cols = (cols & 1) * (COLS // 2) + (cols >> 1)
     slots = jnp.arange(SLOTS, dtype=i32)
     lives = slots < block_count[0]
     hot = (rows[:, None] == jnp.arange(ROWS, dtype=i32)[None, :]) & lives[:, None]
@@ -500,9 +512,8 @@
     has = (groups > 0).astype(f32)
     upper = (block_atoms >= 256).astype(i32)
     digits = jnp.concatenate([block_atoms - 256 * upper, upper], axis=1).astype(bf16)
-    dict_t = jnp.pad(dictionary.T, ((0, 0), (0, ATOMPAD - ATOMS)))
-    w_in = initial_weights.reshape(2, 256, BF)
-    w_in = jnp.concatenate([w_in[0], w_in[1]], axis=1)
+    words = jnp.pad(dictionary, ((0, ATOMPAD - ATOMS), (0, 128 - DIRS)))
+    w_in = initial_weights.reshape(COLS // 2, 2 * BF)
     sig_in = jnp.pad(signal.reshape(8, 8, DIRS), ((0, 0), (0, 0), (0, 128 - DIRS)))
 
     smem = pl.BlockSpec(memory_space=pltpu.SMEM)
@@ -512,7 +523,7 @@
         kernel,
         out_shape=(
             jax.ShapeDtypeStruct((256, 128), f32),
-            jax.ShapeDtypeStruct((NF, 8, 128), f32),
+            jax.ShapeDtypeStruct((ROWS // 2, 8, DIRS), f32),
         ),
         in_specs=[smem] * 4 + [pl.BlockSpec(memory_space=pl.ANY)] + [vmem] * 7,
         out_specs=(vmem, vmem),
@@ -520,6 +531,7 @@
             pltpu.VMEM((SLOTS, BV * BF), bf16),
             pltpu.VMEM((2, BV * GPAD, 128), f32),
             pltpu.VMEM((SPAD, SLOTS), bf16),
+            pltpu.VMEM((DIRS, ATOMPAD), bf16),
             pltpu.VMEM((GPAD, 256), f32),
             pltpu.VMEM((GROUPS, BV, 256), bf16),
             pltpu.VMEM((2, GROUPS, HALF, 256), bf16),
@@ -564,16 +576,14 @@
         has,
         coefficients,
         digits,
-        dict_t,
+        words,
         place[None, :],
         cols[None, :],
         cols[:, None],
         w_in,
         sig_in,
     )
-    weights = jnp.concatenate([w_new[:, :BF], w_new[:, BF:]], axis=0).reshape(-1)
-    res = res[:, :, :HALF].reshape(8, 2, 8, 2, PIECE).transpose(0, 2, 3, 1, 4)
-    return (weights, res.reshape(ROWS, 4 * DIRS))
+    return (w_new.reshape(-1), res.reshape(ROWS, 4 * DIRS))
 
 
 def solution(mesh):

time: 239 us -> 239 us (level)
    unnamed x3 -> x5, local copies, waits for them, and re-layouts: 0.94 us -> 3.5 us
where the time goes in v6:
time: 239 us; the launch traced here: 238 us
  Pallas kernels  229 us (96%)
  local copies, waits for them, and re-layouts  5.16 us (2%)
    pallas_call x1, Pallas kernels, local(): pl.pallas_call(kernel, out_shape=(jax.ShapeDtypeStruct((256, 128), f32),...  229 us

profile of v6, /device:TPU:0, one launch (start us, length us, event | category | flops | bytes accessed | tf_op | source)
XLA Modules:
  0.0 237.9 jit_solution(15659712173253864449)
XLA Ops:
  1.3 0.7 broadcast_and_fusion
  2.0 0.1 convert_reduce_fusion.1
  2.1 0.1 select_reduce_fusion.1
  2.2 0.1 convert_reduce_fusion.2
  2.4 0.1 fusion.4
  2.5 0.1 select_reduce_fusion
  2.5 0.2 convert_reduce_fusion
  2.7 0.7 shift-right-arithmetic_add_fusion
  3.4 0.8 reshape.80
  4.3 1.0 copy.19
  5.3 0.9 copy.18
  6.3 0.1 pad_maximum_fusion.digits
  6.4 0.1 copy.20.cols_sub
  6.5 0.0 copy-start
  6.5 0.9 copy-done
  7.4 229.2 %shard_map.95 = (f32[256,128]{1,0:T(8,128)S(1)}, f32[8,8,96]{2,1,0:T(8,128)S(1)}) custom-call(s32[80]{0:T(128)S(1)} %broadcast_minimum_fusion.grow, s32[16]{0:T(128)S(1)} %get-tuple-element.9.last, f32[80]{0:T(128)S(1)} %convert_subtract_fusion.keep, f32[16]{0:T(128)S(1)} %get-tuple-element.6.has, bf16[256,4096]{1,0:T(8,128)(2,1)} %coef_hbm.1, ...), custom_call_target="tpu_custom_call" | custom-call | tf_op jit(solution)/shard_map/pallas_call | solution.py:522
  236.6 0.7 reshape.82
  237.3 0.7 copy.23
  (12 shorter events, 0.1 us)
Async XLA Ops:
  6.5 0.9 copy-start

commit v7 on v6

--- a/solution.py
+++ b/solution.py
@@ -63,16 +63,20 @@
     keep,
     has,
     coef_hbm,
-    digits,
-    words,
+    atoms_hbm,
+    words_hbm,
+    cols_hbm,
+    w_hbm,
     place_lane,
-    cols_lane,
-    cols_sub,
-    w_in,
     sig_in,
     w_out,
     res_out,
     coef,
+    atoms,
+    words,
+    cols,
+    w_in,
+    wordpad,
     wide,
     pick,
     dict_t,
@@ -117,15 +121,21 @@
     r_fin,
     s_two,
     r_twin,
-    s_coef,
+    s_get,
 ):
     me_v = lax.axis_index("vox")
     me_f = lax.axis_index("fas")
     me_c = lax.rem(me_v, 2)
     me_y = me_v // 2
     twin = me_v + 1 - 2 * me_c
-    fetch = pltpu.make_async_copy(coef_hbm, coef, s_coef)
-    fetch.start()
+    fetches = [
+        pltpu.make_async_copy(src, dst, s_get.at[k])
+        for k, (src, dst) in enumerate(
+            ((atoms_hbm, atoms), (words_hbm, words), (cols_hbm, cols), (w_hbm, w_in), (coef_hbm, coef))
+        )
+    ]
+    for fetch in fetches:
+        fetch.start()
 
     def remote(src, dst, send_sem, recv_sem, device):
         return pltpu.make_async_remote_copy(
@@ -195,7 +205,15 @@
         hot = (place_lane[...] == turn_row + q).astype(f32).astype(bf16)
         pick[q * GPAD : (q + 1) * GPAD, :] = hot
     pick[QUAD * GPAD :, :] = jnp.zeros((SPAD - QUAD * GPAD, SLOTS), bf16)
-    found = jnp.dot(pick[0 : QUAD * GPAD, :], digits[...], preferred_element_type=f32)
+    wordpad[...] = jnp.zeros_like(wordpad)
+    for fetch in fetches[:4]:
+        fetch.wait()
+    upper = jnp.where(atoms[...] >= 256, 1, 0)
+    digits = jnp.concatenate(
+        [(atoms[...] - 256 * upper).astype(f32), upper.astype(f32)], axis=1
+    ).astype(bf16)
+    found = jnp.dot(pick[0 : QUAD * GPAD, :], digits, preferred_element_type=f32)
+    wordpad[0:ATOMS, 0:DIRS] = words[...].astype(f32)
     found = jnp.where(low_lanes(found.shape), found, found * 256.0)
     found = fold(found)
     mask = low_lanes((GPAD, 128))
@@ -203,7 +221,7 @@
     names[:, 128:256] = jnp.where(mask, found[2 * GPAD : 3 * GPAD], found[3 * GPAD :])
 
     for k in range(ATOMPAD // 128):
-        block = jnp.transpose(words[k * 128 : (k + 1) * 128, :].astype(f32))
+        block = jnp.transpose(wordpad[k * 128 : (k + 1) * 128, :])
         dict_t[:, k * 128 : (k + 1) * 128] = block[:DIRS].astype(bf16)
 
     def name_atoms(g, carry):
@@ -215,13 +233,15 @@
         return carry
 
     lax.fori_loop(0, GROUPS, name_atoms, 0, unroll=19)
-    where_col = (lax.broadcasted_iota(jnp.int32, (COLS, SLOTS), 0) == cols_lane[...]).astype(f32)
+    col = cols[...] & (COLS - 1)
+    col = (col & 1) * (COLS // 2) + lax.shift_right_logical(col, 1)
+    where_col = (lax.broadcasted_iota(jnp.int32, (COLS, SLOTS), 0) == col).astype(f32).astype(bf16)
+    both_lanes = (((1,), (1,)), ((), ()))
     sel[...] = lax.dot_general(
-        where_col.astype(bf16), pick[...], (((1,), (1,)), ((), ())), preferred_element_type=f32
+        where_col, pick[...], both_lanes, preferred_element_type=f32
     ).astype(bf16)
-    where_col = (lax.broadcasted_iota(jnp.int32, (SLOTS, COLS), 1) == cols_sub[...]).astype(f32)
-    sel_t[...] = jnp.dot(
-        pick[...], where_col.astype(bf16), preferred_element_type=f32
+    sel_t[...] = lax.dot_general(
+        pick[...], where_col, both_lanes, preferred_element_type=f32
     ).astype(bf16)
     contrib[...] = jnp.zeros_like(contrib)
     b_two[...] = jnp.zeros_like(b_two)
@@ -230,7 +250,7 @@
     start_sig, wait_sig, sent_sig = copies(lambda p: sig_in.at[p // 2], sg_in, s_sig, r_sig)
     start_sig()
 
-    fetch.wait()
+    fetches[4].wait()
 
     def spread(t, carry):
         at_lane = pl.multiple_of(t * 128, 128)
@@ -489,8 +509,6 @@
 ):
     i32 = jnp.int32
     rows = block_rows & (ROWS - 1)
-    cols = block_cols & (COLS - 1)
-    cols = (cols & 1) * (COLS // 2) + (cols >> 1)
     slots = jnp.arange(SLOTS, dtype=i32)
     lives = slots < block_count[0]
     hot = (rows[:, None] == jnp.arange(ROWS, dtype=i32)[None, :]) & lives[:, None]
@@ -510,10 +528,6 @@
     keep = 1.0 - is_first.astype(f32)
     last = jnp.maximum(ends - 1, 0)
     has = (groups > 0).astype(f32)
-    upper = (block_atoms >= 256).astype(i32)
-    digits = jnp.concatenate([block_atoms - 256 * upper, upper], axis=1).astype(bf16)
-    words = jnp.pad(dictionary, ((0, ATOMPAD - ATOMS), (0, 128 - DIRS)))
-    w_in = initial_weights.reshape(COLS // 2, 2 * BF)
     sig_in = jnp.pad(signal.reshape(8, 8, DIRS), ((0, 0), (0, 0), (0, 128 - DIRS)))
 
     smem = pl.BlockSpec(memory_space=pltpu.SMEM)
@@ -525,10 +539,15 @@
             jax.ShapeDtypeStruct((256, 128), f32),
             jax.ShapeDtypeStruct((ROWS // 2, 8, DIRS), f32),
         ),
-        in_specs=[smem] * 4 + [pl.BlockSpec(memory_space=pl.ANY)] + [vmem] * 7,
+        in_specs=[smem] * 4 + [pl.BlockSpec(memory_space=pl.ANY)] * 5 + [vmem] * 2,
         out_specs=(vmem, vmem),
         scratch_shapes=[
             pltpu.VMEM((SLOTS, BV * BF), bf16),
+            pltpu.VMEM((SLOTS, BF), jnp.int32),
+            pltpu.VMEM((ATOMS, DIRS), bf16),
+            pltpu.VMEM((1, SLOTS), jnp.int32),
+            pltpu.VMEM((COLS // 2, 2 * BF), f32),
+            pltpu.VMEM((ATOMPAD, 128), f32),
             pltpu.VMEM((2, BV * GPAD, 128), f32),
             pltpu.VMEM((SPAD, SLOTS), bf16),
             pltpu.VMEM((DIRS, ATOMPAD), bf16),
@@ -565,7 +584,7 @@
             for n in ((NF,), (2, NF), (2, NF), (2, SIDE), (CHIPS,), (NF,), (5,))
             for _ in range(2)
         ]
-        + [dma(())],
+        + [dma((5,))],
         compiler_params=pltpu.CompilerParams(
             collective_id=0, has_side_effects=True, vmem_limit_bytes=52 * 1024 * 1024
         ),
@@ -575,12 +594,11 @@
         keep,
         has,
         coefficients,
-        digits,
-        words,
+        block_atoms,
+        dictionary,
+        block_cols[None, :],
+        initial_weights.reshape(COLS // 2, 2 * BF),
         place[None, :],
-        cols[None, :],
-        cols[:, None],
-        w_in,
         sig_in,
     )
     return (w_new.reshape(-1), res.reshape(ROWS, 4 * DIRS))

time: 239 us -> 239 us (level)
  no operation moved by 1% of the time
where the time goes in v7:
time: 239 us; the launch traced here: 238 us
  Pallas kernels  230 us (96%)
  local copies, waits for them, and re-layouts  5.68 us (2%)
    pallas_call x1, Pallas kernels, local(): pl.pallas_call(kernel, out_shape=(jax.ShapeDtypeStruct((256, 128), f32),...  230 us

profile of v7, /device:TPU:0, one launch (start us, length us, event | category | flops | bytes accessed | tf_op | source)
XLA Modules:
  0.0 238.4 jit_solution(9037204719592094305)
XLA Ops:
  1.3 0.7 broadcast_and_fusion
  2.0 0.1 convert_reduce_fusion.1
  2.1 0.1 select_reduce_fusion.1
  2.2 0.1 convert_reduce_fusion.2
  2.4 0.1 fusion.4
  2.5 0.1 select_reduce_fusion
  2.5 0.2 convert_reduce_fusion
  2.7 0.8 reshape.80
  3.6 1.0 copy.13.words_hbm
  4.6 0.9 copy.12.atoms_hbm
  5.5 0.0 copy-start
  5.5 0.9 copy-done
  6.4 0.0 copy-start.1
  6.4 0.7 copy-done.1
  7.1 230.0 %shard_map.95 = (f32[256,128]{1,0:T(8,128)S(1)}, f32[8,8,96]{2,1,0:T(8,128)S(1)}) custom-call(s32[80]{0:T(128)S(1)} %broadcast_minimum_fusion.grow, s32[16]{0:T(128)S(1)} %get-tuple-element.9.last, f32[80]{0:T(128)S(1)} %convert_subtract_fusion.keep, f32[16]{0:T(128)S(1)} %get-tuple-element.6.has, bf16[256,4096]{1,0:T(8,128)(2,1)} %coef_hbm.1, ...), custom_call_target="tpu_custom_call" | custom-call | tf_op jit(solution)/shard_map/pallas_call | solution.py:536
  237.1 0.7 reshape.82
  237.8 0.7 copy.16
  (9 shorter events, 0.1 us)
Async XLA Ops:
  5.5 0.9 copy-start
  6.4 0.7 copy-start.1

commit v8 on v7

--- a/solution.py
+++ b/solution.py
@@ -67,8 +67,8 @@
     words_hbm,
     cols_hbm,
     w_hbm,
-    place_lane,
-    sig_in,
+    place_hbm,
+    sig_hbm,
     w_out,
     res_out,
     coef,
@@ -76,7 +76,8 @@
     words,
     cols,
     w_in,
-    wordpad,
+    place_lane,
+    sig_in,
     wide,
     pick,
     dict_t,
@@ -131,7 +132,15 @@
     fetches = [
         pltpu.make_async_copy(src, dst, s_get.at[k])
         for k, (src, dst) in enumerate(
-            ((atoms_hbm, atoms), (words_hbm, words), (cols_hbm, cols), (w_hbm, w_in), (coef_hbm, coef))
+            (
+                (place_hbm, place_lane),
+                (atoms_hbm, atoms),
+                (words_hbm, words),
+                (cols_hbm, cols),
+                (w_hbm, w_in),
+                (sig_hbm, sig_in),
+                (coef_hbm, coef),
+            )
         )
     ]
     for fetch in fetches:
@@ -200,29 +209,29 @@
             device_id_type=pl.DeviceIdType.MESH,
         )
 
+    for fetch in fetches[:6]:
+        fetch.wait()
     turn_row = lax.broadcasted_iota(jnp.int32, (GPAD, SLOTS), 0) * QUAD
     for q in range(QUAD):
         hot = (place_lane[...] == turn_row + q).astype(f32).astype(bf16)
         pick[q * GPAD : (q + 1) * GPAD, :] = hot
     pick[QUAD * GPAD :, :] = jnp.zeros((SPAD - QUAD * GPAD, SLOTS), bf16)
-    wordpad[...] = jnp.zeros_like(wordpad)
-    for fetch in fetches[:4]:
-        fetch.wait()
     upper = jnp.where(atoms[...] >= 256, 1, 0)
     digits = jnp.concatenate(
-        [(atoms[...] - 256 * upper).astype(f32), upper.astype(f32)], axis=1
+        [(atoms[...] - 256 * upper).astype(f32), upper.astype(f32)], axis=0
     ).astype(bf16)
-    found = jnp.dot(pick[0 : QUAD * GPAD, :], digits, preferred_element_type=f32)
-    wordpad[0:ATOMS, 0:DIRS] = words[...].astype(f32)
+    both_lanes = (((1,), (1,)), ((), ()))
+    found = lax.dot_general(
+        pick[0 : QUAD * GPAD, :], digits, both_lanes, preferred_element_type=f32
+    )
     found = jnp.where(low_lanes(found.shape), found, found * 256.0)
     found = fold(found)
     mask = low_lanes((GPAD, 128))
     names[:, 0:128] = jnp.where(mask, found[0:GPAD], found[GPAD : 2 * GPAD])
     names[:, 128:256] = jnp.where(mask, found[2 * GPAD : 3 * GPAD], found[3 * GPAD :])
 
-    for k in range(ATOMPAD // 128):
-        block = jnp.transpose(wordpad[k * 128 : (k + 1) * 128, :])
-        dict_t[:, k * 128 : (k + 1) * 128] = block[:DIRS].astype(bf16)
+    dict_t[...] = jnp.zeros_like(dict_t)
+    dict_t[:, 0:ATOMS] = words[...]
 
     def name_atoms(g, carry):
         row = names[pl.ds(g, 1), :].astype(jnp.int32)
@@ -236,7 +245,6 @@
     col = cols[...] & (COLS - 1)
     col = (col & 1) * (COLS // 2) + lax.shift_right_logical(col, 1)
     where_col = (lax.broadcasted_iota(jnp.int32, (COLS, SLOTS), 0) == col).astype(f32).astype(bf16)
-    both_lanes = (((1,), (1,)), ((), ()))
     sel[...] = lax.dot_general(
         where_col, pick[...], both_lanes, preferred_element_type=f32
     ).astype(bf16)
@@ -250,7 +258,7 @@
     start_sig, wait_sig, sent_sig = copies(lambda p: sig_in.at[p // 2], sg_in, s_sig, r_sig)
     start_sig()
 
-    fetches[4].wait()
+    fetches[6].wait()
 
     def spread(t, carry):
         at_lane = pl.multiple_of(t * 128, 128)
@@ -539,15 +547,16 @@
             jax.ShapeDtypeStruct((256, 128), f32),
             jax.ShapeDtypeStruct((ROWS // 2, 8, DIRS), f32),
         ),
-        in_specs=[smem] * 4 + [pl.BlockSpec(memory_space=pl.ANY)] * 5 + [vmem] * 2,
+        in_specs=[smem] * 4 + [pl.BlockSpec(memory_space=pl.ANY)] * 7,
         out_specs=(vmem, vmem),
         scratch_shapes=[
             pltpu.VMEM((SLOTS, BV * BF), bf16),
-            pltpu.VMEM((SLOTS, BF), jnp.int32),
-            pltpu.VMEM((ATOMS, DIRS), bf16),
+            pltpu.VMEM((BF, SLOTS), jnp.int32),
+            pltpu.VMEM((DIRS, ATOMS), bf16),
             pltpu.VMEM((1, SLOTS), jnp.int32),
             pltpu.VMEM((COLS // 2, 2 * BF), f32),
-            pltpu.VMEM((ATOMPAD, 128), f32),
+            pltpu.VMEM((1, SLOTS), jnp.int32),
+            pltpu.VMEM((NF // 2, 8, 128), f32),
             pltpu.VMEM((2, BV * GPAD, 128), f32),
             pltpu.VMEM((SPAD, SLOTS), bf16),
             pltpu.VMEM((DIRS, ATOMPAD), bf16),
@@ -584,9 +593,9 @@
             for n in ((NF,), (2, NF), (2, NF), (2, SIDE), (CHIPS,), (NF,), (5,))
             for _ in range(2)
         ]
-        + [dma((5,))],
+        + [dma((7,))],
         compiler_params=pltpu.CompilerParams(
-            collective_id=0, has_side_effects=True, vmem_limit_bytes=52 * 1024 * 1024
+            collective_id=0, has_side_effects=True, vmem_limit_bytes=64 * 1024 * 1024
         ),
     )(
         grow,
@@ -594,8 +603,8 @@
         keep,
         has,
         coefficients,
-        block_atoms,
-        dictionary,
+        block_atoms.T,
+        dictionary.T,
         block_cols[None, :],
         initial_weights.reshape(COLS // 2, 2 * BF),
         place[None, :],

time: 239 us -> 241 us (level)
  other arithmetic: 1.43 us -> 4.19 us
    unnamed x7 -> x1, local copies, waits for them, and re-layouts: 4.18 us -> 1.57 us
where the time goes in v8:
time: 241 us
  Pallas kernels  231 us (96%)
  local copies, waits for them, and re-layouts  4.44 us (2%)
  other arithmetic  4.19 us (2%)
    pallas_call x1, Pallas kernels, local(): pl.pallas_call(kernel, out_shape=(jax.ShapeDtypeStruct((256, 128), f32),...  231 us

profile of v8, /device:TPU:0, one launch (start us, length us, event | category | flops | bytes accessed | tf_op | source)
XLA Modules:
  0.0 240.5 jit_solution(9250522273593227891)
XLA Ops:
  1.3 0.7 broadcast_and_fusion
  2.0 0.1 convert_reduce_fusion.1
  2.1 0.6 fusion.5
  2.7 0.1 select_reduce_fusion.1
  2.8 0.1 convert_reduce_fusion.2
  2.9 0.5 broadcast_minimum_fusion.grow
  3.4 0.6 fusion.6
  4.0 0.1 fusion.4
  4.1 0.5 convert_subtract_fusion.keep
  4.6 0.1 select_reduce_fusion
  4.7 0.2 convert_reduce_fusion
  4.9 0.6 compare_select_fusion.place_hbm
  5.5 0.8 reshape.80
  6.3 0.6 pad.4.sig_hbm
  6.9 230.6 %shard_map.95 = (f32[256,128]{1,0:T(8,128)}, f32[8,8,96]{2,1,0:T(8,128)}) custom-call(s32[80]{0:T(128)} %broadcast_minimum_fusion.grow, s32[16]{0:T(128)} %get-tuple-element.9.last, f32[80]{0:T(128)} %convert_subtract_fusion.keep, f32[16]{0:T(128)} %get-tuple-element.6.has, bf16[256,4096]{1,0:T(8,128)(2,1)} %coef_hbm.1, s32[64,256]{1,0:T(8,128)} %bitcast.12, ...), custom_call_target="tpu_custom_call" | custom-call | tf_op jit(solution)/shard_map/pallas_call | solution.py:544
  237.5 1.4 reshape.82
  239.0 1.6 copy.12
  (3 shorter events, 0.0 us)

commit v9 on v8

--- a/solution.py
+++ b/solution.py
@@ -595,7 +595,7 @@
         ]
         + [dma((7,))],
         compiler_params=pltpu.CompilerParams(
-            collective_id=0, has_side_effects=True, vmem_limit_bytes=64 * 1024 * 1024
+            collective_id=0, has_side_effects=True, vmem_limit_bytes=52 * 1024 * 1024
         ),
     )(
         grow,

time: 241 us -> 239 us (level)
  other arithmetic: 4.19 us -> 1.43 us
where the time goes in v9:
time: 239 us; the launch traced here: 238 us
  Pallas kernels  230 us (96%)
  local copies, waits for them, and re-layouts  5.47 us (2%)
    pallas_call x1, Pallas kernels, local(): pl.pallas_call(kernel, out_shape=(jax.ShapeDtypeStruct((256, 128), f32),...  230 us

profile of v9, /device:TPU:0, one launch (start us, length us, event | category | flops | bytes accessed | tf_op | source)
XLA Modules:
  0.0 237.9 jit_solution(15864886391904529932)
XLA Ops:
  1.3 0.7 broadcast_and_fusion
  2.0 0.1 convert_reduce_fusion.1
  2.1 0.1 select_reduce_fusion.1
  2.2 0.1 convert_reduce_fusion.2
  2.4 0.1 fusion.4
  2.5 0.1 select_reduce_fusion
  2.5 0.2 convert_reduce_fusion
  2.7 0.8 reshape.80
  3.6 0.0 copy-start
  3.6 0.9 copy-done
  4.5 0.0 copy-start.1
  4.5 0.9 copy-done.1
  5.4 0.0 copy-start.2
  5.4 0.8 copy-done.2
  6.2 0.0 copy-start.3
  6.2 0.7 copy-done.3
  6.9 229.7 %shard_map.95 = (f32[256,128]{1,0:T(8,128)S(1)}, f32[8,8,96]{2,1,0:T(8,128)S(1)}) custom-call(s32[80]{0:T(128)S(1)} %broadcast_minimum_fusion.grow, s32[16]{0:T(128)S(1)} %get-tuple-element.9.last, f32[80]{0:T(128)S(1)} %convert_subtract_fusion.keep, f32[16]{0:T(128)S(1)} %get-tuple-element.6.has, bf16[256,4096]{1,0:T(8,128)(2,1)} %coef_hbm.1, ...), custom_call_target="tpu_custom_call" | custom-call | tf_op jit(solution)/shard_map/pallas_call | solution.py:544
  236.5 0.7 reshape.82
  237.2 0.7 copy.12
  (9 shorter events, 0.1 us)
Async XLA Ops:
  3.6 0.9 copy-start
  4.5 0.9 copy-start.1
  5.4 0.8 copy-start.2
  6.2 0.7 copy-start.3
